TPU v7x, 512 devices: a whole 4x4x16 slice. The times are simulated.
512 devices in a mesh: rep: 16 (over z), gx: 4 (over x_lo, core), gy: 8 (over y, x_hi).
Axes of the slice: x: 4 (x_hi: 2, x_lo: 2; x = x_hi * 2 + x_lo), y: 4, z: 16, core: 2. Of those that a mesh axis runs over, the one named last changes fastest.
Arguments:
- velocity: bfloat16 [16, 128, 256, 128], P('rep', 'gx', 'gy'), may hold values from -1.5 to 1.5
- tracers: bfloat16 [16, 128, 256, 128], P('rep', 'gx', 'gy'), may hold values from 0.5 to 2
- forcing: bfloat16 [48, 128, 256, 128], P('rep', 'gx', 'gy'), may hold values from -6 to 6
- coefficients: float32 [48], P('rep'), may hold values from -1.2 to 1.2
- land_mask: int32 [128, 256], P('gx', 'gy'), may hold values 0 or 1
- step_levels: int32 [3], replicated, may hold values from 0 to 15
Outputs:
- combined: float32 [128, 256, 128], P(('gx', 'rep'), 'gy')
- adjoints: float32 [48, 128, 256, 128], P('rep', 'gx', 'gy')
Inputs may be any that keep to these rules, and one draw needn't show every extreme that they name: `step_levels`: each entry names the group along rep that stores the level.
All inputs are finite; a program needn't handle non-finite values. No bound on the sum of `land_mask` on one device may be relied on, other than what follows from the above.
Results may differ from a plain program's by a relative error of at most 0.0003.
Values may be sent and summed in bfloat16 or wider, within the bound.
No kernel may reach another device: no remote copies, remote signals or barrier semaphores. Data moves between devices by JAX's collectives and lax.ppermute only.
A program may use at most 64 MiB of HBM per device.

v0:
```python
import jax
import jax.numpy as jnp
from jax import lax
from jax.sharding import PartitionSpec as P

STEPS = 3


time_step = 0.1


def extended(cells, sides, width):
    for axis, dim in sides:
        count = lax.axis_size(axis)
        ends = count - 1
        head = lax.slice_in_dim(cells, 0, width, axis=dim)
        tail = lax.slice_in_dim(cells, cells.shape[dim] - width, cells.shape[dim], axis=dim)
        cells = jnp.concatenate(
            [
                lax.ppermute(tail, axis, [(i, (i + 1) % count) for i in range(ends)]),
                cells,
                lax.ppermute(head, axis, [((i + 1) % count, i) for i in range(ends)]),
            ],
            axis=dim,
        )
    return cells


def spread_2(x, axis, root):
    mine = lax.axis_index(axis) == root
    return lax.psum(jnp.where(mine, x, jnp.zeros_like(x)), axis)


def advance(state, speed_ext, tracer, ocean):
    half = state.shape[-1] // 2
    padded = extended(state, (("gx", 1), ("gy", 2)), 1)
    speed = speed_ext.astype(jnp.float32)
    along_x = jnp.concatenate([speed[..., :half], speed[..., :half]], axis=-1)[None]
    along_y = jnp.concatenate([speed[..., half:], speed[..., half:]], axis=-1)[None]
    east = along_x * padded
    north = along_y * padded
    advect = 0.5 * (east[:, :-2, 1:-1] - east[:, 2:, 1:-1]) + 0.5 * (
        north[:, 1:-1, :-2] - north[:, 1:-1, 2:]
    )
    spread = (
        padded[:, :-2, 1:-1]
        + padded[:, 2:, 1:-1]
        + padded[:, 1:-1, :-2]
        + padded[:, 1:-1, 2:]
        - 4.0 * state
    )
    tracer_f = tracer.astype(jnp.float32)[None]
    mixing = tracer_f[..., :half] * state[..., :half] - tracer_f[..., half:] * state[..., half:]
    exchange = jnp.concatenate([-mixing, mixing], axis=-1)
    return ocean * (state + time_step * (advect + spread + exchange))


def local(velocity, tracers, forcing, coefficients, land_mask, step_levels):
    ocean = land_mask.astype(jnp.float32)[None, :, :, None]
    state = forcing.astype(jnp.float32)
    own_speed = velocity[0]
    own_tracer = tracers[0]
    for step in range(STEPS):
        owner = step_levels[step]
        speed, tracer = (spread_2(own_speed, "rep", owner), spread_2(own_tracer, "rep", owner))
        speed_ext = extended(speed, (("gx", 0), ("gy", 1)), 1)
        state = advance(state, speed_ext, tracer, ocean)
    weighted = jnp.sum(coefficients[:, None, None, None] * state, axis=0)
    total = lax.psum(weighted, "rep")
    owned = weighted.shape[0] // lax.axis_size("rep")
    return (lax.dynamic_slice_in_dim(total, lax.axis_index("rep") * owned, owned, 0), state)


def solution(mesh):
    placed = (
        P("rep", "gx", "gy", None),
        P("rep", "gx", "gy", None),
        P("rep", "gx", "gy", None),
        P("rep"),
        P("gx", "gy"),
        P(),
    )
    return jax.shard_map(
        local,
        mesh=mesh,
        in_specs=placed,
        out_specs=(P(("gx", "rep"), "gy", None), P("rep", "gx", "gy", None)),
        check_vma=False,
    )
```

profile of v0, /device:TPU:2, one launch (start us, length us, event | category | flops | bytes accessed | tf_op | source)
XLA Modules:
  0.0 403.3 jit_solution(4621567571779690120)
XLA Ops:
  7.2 1.4 fusion.61
  10.6 1.9 select_bitcast_fusion
  12.5 2.0 broadcast_select_fusion
  14.6 1.9 collective-permute-start.5
  16.5 2.4 collective-permute-start.4
  19.1 7.0 %collective-permute-done.4 = f32[3,1,32,128]{3,2,1,0:T(8,128)S(1)} collective-permute-done((f32[3,1,32,128]{3,2,1,0:T(8,128)S(1)}, f32[3,1,32,128]{3,2,1,0:T(8,128)S(1)}, u32[]{:S(2)}, u32[]{:S(2)}) %collective-permute-start.4) | collective-permute-done | bytes 49184 | tf_op jit(solution)/shard_map/ppermute | solution.py:20
  26.2 1.3 collective-permute-start.7
  27.5 6.1 %collective-permute-start.6 = (f32[3,34,1,128]{3,2,1,0:T(1,128)S(1)}, f32[3,34,1,128]{3,2,1,0:T(1,128)S(1)}, u32[]{:S(2)}, u32[]{:S(2)}) collective-permute-start(f32[3,34,1,128]{3,2,1,0:T(1,128)S(1)} %get-tuple-element.26), channel_id=1, source_target_pairs={{0,1},{1,2},{2,3},{3,4},{4,5},{5,6},{6,7},{8,9},{9,10},{10,11},{11... | collective-permute-start | bytes 156680 | tf_op jit(solution)/shard_map/ppermute | solution.py:20
  33.6 128.3 %all-reduce.6.cloned.1.call-done = (bf16[32,32,128]{2,1,0:T(8,128)(2,1)}, bf16[1,32,32,128]{3,2,1,0:T(8,128)(2,1)}, bf16[32,32,128]{2,1,0:T(8,128)(2,1)}, bf16[1...) async-done(((bf16[32,32,128]{2,1,0:T(8,128)(2,1)}, bf16[1,32,32,128]{3,2,1,0:T(8,128)(2,1)}, ...) | async-done | bytes 1572880 | tf_op jit(solution)/shard_map/psum | solution.py:31
  161.9 0.8 fusion.60
  162.7 1.9 collective-permute-start
  164.6 3.6 collective-permute-start.1
  168.3 1.0 broadcast_in_dim.27
  169.5 2.1 collective-permute-start.8
  172.2 0.6 fusion.47
  173.1 3.6 collective-permute-start.9
  176.8 1.9 collective-permute-start.16
  178.8 3.6 collective-permute-start.17
  182.5 1.3 collective-permute-start.3
  183.9 6.1 %collective-permute-start.2 = (bf16[34,1,128]{2,1,0:T(2,128)(2,1)S(1)}, bf16[34,1,128]{2,1,0:T(2,128)(2,1)S(1)}, u32[]{:S(2)}, u32[]{:S(2)}) collective-permute-start(bf16[34,1,128]{2,1,0:T(2,128)(2,1)S(1)} %get-tuple-element.50), channel_id=1, source_target_pairs={{0,1},{1,2},{2,3},{3,4},{4,5},{5,6},{6,7},{8,9},{9,10},{10,11},{11... | collective-permute-start | bytes 26120 | tf_op jit(solution)/shard_map/ppermute | solution.py:20
  190.0 1.3 collective-permute-start.11
  191.4 6.1 %collective-permute-start.10 = (bf16[34,1,128]{2,1,0:T(2,128)(2,1)S(1)}, bf16[34,1,128]{2,1,0:T(2,128)(2,1)S(1)}, u32[]{:S(2)}, u32[]{:S(2)}) collective-permute-start(bf16[34,1,128]{2,1,0:T(2,128)(2,1)S(1)} %get-tuple-element.48), channel_id=1, source_target_pairs={{0,1},{1,2},{2,3},{3,4},{4,5},{5,6},{6,7},{8,9},{9,10},{10,11},{11... | collective-permute-start | bytes 26120 | tf_op jit(solution)/shard_map/ppermute | solution.py:20
  197.4 1.3 collective-permute-start.19
  199.1 0.4 pad_maximum_fusion.27
  199.6 6.4 %collective-permute-start.18 = (bf16[34,1,128]{2,1,0:T(2,128)(2,1)S(1)}, bf16[34,1,128]{2,1,0:T(2,128)(2,1)S(1)}, u32[]{:S(2)}, u32[]{:S(2)}) collective-permute-start(bf16[34,1,128]{2,1,0:T(2,128)(2,1)S(1)} %get-tuple-element.46), channel_id=1, source_target_pairs={{0,1},{1,2},{2,3},{3,4},{4,5},{5,6},{6,7},{8,9},{9,10},{10,11},{11... | collective-permute-start | bytes 26120 | tf_op jit(solution)/shard_map/ppermute | solution.py:20
  206.0 0.4 fusion.41
  206.5 3.4 fusion.31
  209.9 1.9 collective-permute-start.13
  211.9 0.6 fusion.45
  212.5 2.4 collective-permute-start.12
  215.7 2.2 collective-permute-done.12
  217.9 1.3 collective-permute-start.15
  219.2 7.3 %collective-permute-start.14 = (f32[3,34,1,128]{3,2,1,0:T(1,128)S(1)}, f32[3,34,1,128]{3,2,1,0:T(1,128)S(1)}, u32[]{:S(2)}, u32[]{:S(2)}) collective-permute-start(f32[3,34,1,128]{3,2,1,0:T(1,128)S(1)} %get-tuple-element.24), channel_id=1, source_target_pairs={{0,1},{1,2},{2,3},{3,4},{4,5},{5,6},{6,7},{8,9},{9,10},{10,11},{11... | collective-permute-start | bytes 156680 | tf_op jit(solution)/shard_map/ppermute | solution.py:20
  227.0 1.3 collective-permute-done.14
  228.4 0.4 fusion.39
  228.8 3.4 fusion.19
  232.3 1.9 collective-permute-start.21
  234.2 2.4 collective-permute-start.20
  236.6 0.5 pad_maximum_fusion.31
  237.1 2.5 collective-permute-done.20
  239.7 1.3 collective-permute-start.23
  241.0 7.6 %collective-permute-start.22 = (f32[3,34,1,128]{3,2,1,0:T(1,128)S(1)}, f32[3,34,1,128]{3,2,1,0:T(1,128)S(1)}, u32[]{:S(2)}, u32[]{:S(2)}) collective-permute-start(f32[3,34,1,128]{3,2,1,0:T(1,128)S(1)} %get-tuple-element.22), channel_id=1, source_target_pairs={{0,1},{1,2},{2,3},{3,4},{4,5},{5,6},{6,7},{8,9},{9,10},{10,11},{11... | collective-permute-start | bytes 156680 | tf_op jit(solution)/shard_map/ppermute | solution.py:20
  248.6 0.6 fusion.43
  249.2 1.0 collective-permute-done.22
  250.2 0.4 fusion.37
  250.9 5.3 %multiply_reduce_fusion = (f32[32,32,128]{2,1,0:T(8,128)}, f32[3,32,32,128]{3,2,1,0:T(8,128)}) fusion(f32[3]{0:T(128)S(1)} %copy-done.7, f32[3,32,32,128]{3,2,1,0:T(8,128)S(1)} %fusion.19, f32[3,32,32,64]{3,2,1,0:T(8,128)S(1)} %get-tuple-element.11, f32[3,32,32,64]{3,2,1,0:T(8,128)S(1)} %get-tuple-element.10, ...), kind=kLoop, calls=%fused_computation.75 | loop fusion | flops 9699328 | bytes 11741196 | tf_op jit(solution)/shard_map/reduce_sum | solution.py:68
  256.1 138.9 %all-reduce.4.cloned.1.call-done = f32[32,32,128]{2,1,0:T(8,128)} async-done(((f32[32,32,128]{2,1,0:T(8,128)}), f32[32,32,128]{2,1,0:T(8,128)}) %all-reduce.4.cloned.1.call-update) | async-done | bytes 524304 | tf_op jit(solution)/shard_map/psum | solution.py:69
  395.0 1.4 constant_dynamic-slice_fusion
  (73 shorter events, 3.8 us)
Async XLA Ops:
  7.2 154.8 %all-reduce.6.cloned.1.call-start = ((), (), s32[]{:S(2)}) async-start(), calls=%async_computation.1 | async-start | bytes 3145728 | tf_op jit(solution)/shard_map/psum | solution.py:31
  12.5 2.0 copy-start
  14.5 4.6 %copy-start.6 = (s32[32,32]{1,0:T(8,128)S(1)}, s32[32,32]{1,0:T(8,128)}, u32[]{:S(2)}) copy-start(s32[32,32]{1,0:T(8,128)} %param.10) | copy-start | bytes 12292
  14.5 380.6 %all-reduce.4.cloned.1.call-start = ((), (), s32[]{:S(2)}) async-start(), calls=%async_computation | async-start | bytes 1048576 | tf_op jit(solution)/shard_map/psum | solution.py:69
  14.6 4.6 %collective-permute-start.5 = (f32[3,1,32,128]{3,2,1,0:T(8,128)S(1)}, f32[3,1,32,128]{3,2,1,0:T(8,128)S(1)}, u32[]{:S(2)}, u32[]{:S(2)}) collective-permute-start(f32[3,1,32,128]{3,2,1,0:T(8,128)S(1)} %get-tuple-element.33), channel_id=1, source_target_pairs={{8,0},{16,8},{24,16},{9,1},{17,9},{25,17},{10,2},{18,10},{26,18},{... | collective-permute-start | bytes 147464 | tf_op jit(solution)/shard_map/ppermute | solution.py:22
  16.5 9.7 %collective-permute-start.4 = (f32[3,1,32,128]{3,2,1,0:T(8,128)S(1)}, f32[3,1,32,128]{3,2,1,0:T(8,128)S(1)}, u32[]{:S(2)}, u32[]{:S(2)}) collective-permute-start(f32[3,1,32,128]{3,2,1,0:T(8,128)S(1)} %get-tuple-element.32), channel_id=1, source_target_pairs={{0,8},{8,16},{16,24},{1,9},{9,17},{17,25},{2,10},{10,18},{18,26},{... | collective-permute-start | bytes 147464 | tf_op jit(solution)/shard_map/ppermute | solution.py:20
  26.2 173.4 %collective-permute-start.7 = (f32[3,34,1,128]{3,2,1,0:T(1,128)S(1)}, f32[3,34,1,128]{3,2,1,0:T(1,128)S(1)}, u32[]{:S(2)}, u32[]{:S(2)}) collective-permute-start(f32[3,34,1,128]{3,2,1,0:T(1,128)S(1)} %get-tuple-element.27), channel_id=1, source_target_pairs={{1,0},{2,1},{3,2},{4,3},{5,4},{6,5},{7,6},{9,8},{10,9},{11,10},{12... | collective-permute-start | bytes 156680 | tf_op jit(solution)/shard_map/ppermute | solution.py:22
  27.5 178.5 %collective-permute-start.6 = (f32[3,34,1,128]{3,2,1,0:T(1,128)S(1)}, f32[3,34,1,128]{3,2,1,0:T(1,128)S(1)}, u32[]{:S(2)}, u32[]{:S(2)}) collective-permute-start(f32[3,34,1,128]{3,2,1,0:T(1,128)S(1)} %get-tuple-element.26), channel_id=1, source_target_pairs={{0,1},{1,2},{2,3},{3,4},{4,5},{5,6},{6,7},{8,9},{9,10},{10,11},{11... | collective-permute-start | bytes 156680 | tf_op jit(solution)/shard_map/ppermute | solution.py:20
  161.9 7.6 %copy-start.2 = (bf16[32,32,128]{2,1,0:T(8,128)(2,1)S(1)}, bf16[32,32,128]{2,1,0:T(8,128)(2,1)}, u32[]{:S(2)}) copy-start(bf16[32,32,128]{2,1,0:T(8,128)(2,1)} %get-tuple-element.4) | copy-start | bytes 786436
  161.9 9.7 %copy-start.5 = (bf16[1,32,32,128]{3,2,1,0:T(8,128)(2,1)S(1)}, bf16[1,32,32,128]{3,2,1,0:T(8,128)(2,1)}, u32[]{:S(2)}) copy-start(bf16[1,32,32,128]{3,2,1,0:T(8,128)(2,1)} %get-tuple-element.5) | copy-start | bytes 786436
  162.7 10.4 %collective-permute-start = (bf16[1,32,128]{2,1,0:T(8,128)(2,1)S(1)}, bf16[1,32,128]{2,1,0:T(8,128)(2,1)S(1)}, u32[]{:S(2)}, u32[]{:S(2)}) collective-permute-start(bf16[1,32,128]{2,1,0:T(8,128)(2,1)S(1)} %get-tuple-element.57), channel_id=1, source_target_pairs={{0,8},{8,16},{16,24},{1,9},{9,17},{17,25},{2,10},{10,18},{18,26},{... | collective-permute-start | bytes 24584 | tf_op jit(solution)/shard_map/ppermute | solution.py:20
  164.6 12.2 %collective-permute-start.1 = (bf16[1,32,128]{2,1,0:T(8,128)(2,1)S(1)}, bf16[1,32,128]{2,1,0:T(8,128)(2,1)S(1)}, u32[]{:S(2)}, u32[]{:S(2)}) collective-permute-start(bf16[1,32,128]{2,1,0:T(8,128)(2,1)S(1)} %get-tuple-element.56), channel_id=1, source_target_pairs={{8,0},{16,8},{24,16},{9,1},{17,9},{25,17},{10,2},{18,10},{26,18},{... | collective-permute-start | bytes 24584 | tf_op jit(solution)/shard_map/ppermute | solution.py:22
  169.5 2.4 copy-start.4
  169.5 9.3 %collective-permute-start.8 = (bf16[1,32,128]{2,1,0:T(8,128)(2,1)S(1)}, bf16[1,32,128]{2,1,0:T(8,128)(2,1)S(1)}, u32[]{:S(2)}, u32[]{:S(2)}) collective-permute-start(bf16[1,32,128]{2,1,0:T(8,128)(2,1)S(1)} %get-tuple-element.55), channel_id=1, source_target_pairs={{0,8},{8,16},{16,24},{1,9},{9,17},{17,25},{2,10},{10,18},{18,26},{... | collective-permute-start | bytes 24584 | tf_op jit(solution)/shard_map/ppermute | solution.py:20
  172.1 1.0 copy-start.1
  172.1 4.6 %copy-start.3 = (bf16[32,32,128]{2,1,0:T(8,128)(2,1)S(1)}, bf16[32,32,128]{2,1,0:T(8,128)(2,1)}, u32[]{:S(2)}) copy-start(bf16[32,32,128]{2,1,0:T(8,128)(2,1)} %get-tuple-element.2) | copy-start | bytes 786436
  173.1 9.4 %collective-permute-start.9 = (bf16[1,32,128]{2,1,0:T(8,128)(2,1)S(1)}, bf16[1,32,128]{2,1,0:T(8,128)(2,1)S(1)}, u32[]{:S(2)}, u32[]{:S(2)}) collective-permute-start(bf16[1,32,128]{2,1,0:T(8,128)(2,1)S(1)} %get-tuple-element.54), channel_id=1, source_target_pairs={{8,0},{16,8},{24,16},{9,1},{17,9},{25,17},{10,2},{18,10},{26,18},{... | collective-permute-start | bytes 24584 | tf_op jit(solution)/shard_map/ppermute | solution.py:22
  176.8 7.1 %collective-permute-start.16 = (bf16[1,32,128]{2,1,0:T(8,128)(2,1)S(1)}, bf16[1,32,128]{2,1,0:T(8,128)(2,1)S(1)}, u32[]{:S(2)}, u32[]{:S(2)}) collective-permute-start(bf16[1,32,128]{2,1,0:T(8,128)(2,1)S(1)} %get-tuple-element.53), channel_id=1, source_target_pairs={{0,8},{8,16},{16,24},{1,9},{9,17},{17,25},{2,10},{10,18},{18,26},{... | collective-permute-start | bytes 24584 | tf_op jit(solution)/shard_map/ppermute | solution.py:20
  178.8 11.2 %collective-permute-start.17 = (bf16[1,32,128]{2,1,0:T(8,128)(2,1)S(1)}, bf16[1,32,128]{2,1,0:T(8,128)(2,1)S(1)}, u32[]{:S(2)}, u32[]{:S(2)}) collective-permute-start(bf16[1,32,128]{2,1,0:T(8,128)(2,1)S(1)} %get-tuple-element.52), channel_id=1, source_target_pairs={{8,0},{16,8},{24,16},{9,1},{17,9},{25,17},{10,2},{18,10},{26,18},{... | collective-permute-start | bytes 24584 | tf_op jit(solution)/shard_map/ppermute | solution.py:22
  182.5 8.8 %collective-permute-start.3 = (bf16[34,1,128]{2,1,0:T(2,128)(2,1)S(1)}, bf16[34,1,128]{2,1,0:T(2,128)(2,1)S(1)}, u32[]{:S(2)}, u32[]{:S(2)}) collective-permute-start(bf16[34,1,128]{2,1,0:T(2,128)(2,1)S(1)} %get-tuple-element.51), channel_id=1, source_target_pairs={{1,0},{2,1},{3,2},{4,3},{5,4},{6,5},{7,6},{9,8},{10,9},{11,10},{12... | collective-permute-start | bytes 26120 | tf_op jit(solution)/shard_map/ppermute | solution.py:22
  183.9 13.5 %collective-permute-start.2 = (bf16[34,1,128]{2,1,0:T(2,128)(2,1)S(1)}, bf16[34,1,128]{2,1,0:T(2,128)(2,1)S(1)}, u32[]{:S(2)}, u32[]{:S(2)}) collective-permute-start(bf16[34,1,128]{2,1,0:T(2,128)(2,1)S(1)} %get-tuple-element.50), channel_id=1, source_target_pairs={{0,1},{1,2},{2,3},{3,4},{4,5},{5,6},{6,7},{8,9},{9,10},{10,11},{11... | collective-permute-start | bytes 26120 | tf_op jit(solution)/shard_map/ppermute | solution.py:20
  190.0 22.4 %collective-permute-start.11 = (bf16[34,1,128]{2,1,0:T(2,128)(2,1)S(1)}, bf16[34,1,128]{2,1,0:T(2,128)(2,1)S(1)}, u32[]{:S(2)}, u32[]{:S(2)}) collective-permute-start(bf16[34,1,128]{2,1,0:T(2,128)(2,1)S(1)} %get-tuple-element.49), channel_id=1, source_target_pairs={{1,0},{2,1},{3,2},{4,3},{5,4},{6,5},{7,6},{9,8},{10,9},{11,10},{12... | collective-permute-start | bytes 26120 | tf_op jit(solution)/shard_map/ppermute | solution.py:22
  191.4 23.5 %collective-permute-start.10 = (bf16[34,1,128]{2,1,0:T(2,128)(2,1)S(1)}, bf16[34,1,128]{2,1,0:T(2,128)(2,1)S(1)}, u32[]{:S(2)}, u32[]{:S(2)}) collective-permute-start(bf16[34,1,128]{2,1,0:T(2,128)(2,1)S(1)} %get-tuple-element.48), channel_id=1, source_target_pairs={{0,1},{1,2},{2,3},{3,4},{4,5},{5,6},{6,7},{8,9},{9,10},{10,11},{11... | collective-permute-start | bytes 26120 | tf_op jit(solution)/shard_map/ppermute | solution.py:20
  197.4 17.8 %collective-permute-start.19 = (bf16[34,1,128]{2,1,0:T(2,128)(2,1)S(1)}, bf16[34,1,128]{2,1,0:T(2,128)(2,1)S(1)}, u32[]{:S(2)}, u32[]{:S(2)}) collective-permute-start(bf16[34,1,128]{2,1,0:T(2,128)(2,1)S(1)} %get-tuple-element.47), channel_id=1, source_target_pairs={{1,0},{2,1},{3,2},{4,3},{5,4},{6,5},{7,6},{9,8},{10,9},{11,10},{12... | collective-permute-start | bytes 26120 | tf_op jit(solution)/shard_map/ppermute | solution.py:22
  199.6 15.7 %collective-permute-start.18 = (bf16[34,1,128]{2,1,0:T(2,128)(2,1)S(1)}, bf16[34,1,128]{2,1,0:T(2,128)(2,1)S(1)}, u32[]{:S(2)}, u32[]{:S(2)}) collective-permute-start(bf16[34,1,128]{2,1,0:T(2,128)(2,1)S(1)} %get-tuple-element.46), channel_id=1, source_target_pairs={{0,1},{1,2},{2,3},{3,4},{4,5},{5,6},{6,7},{8,9},{9,10},{10,11},{11... | collective-permute-start | bytes 26120 | tf_op jit(solution)/shard_map/ppermute | solution.py:20
  209.9 5.8 %collective-permute-start.13 = (f32[3,1,32,128]{3,2,1,0:T(8,128)S(1)}, f32[3,1,32,128]{3,2,1,0:T(8,128)S(1)}, u32[]{:S(2)}, u32[]{:S(2)}) collective-permute-start(f32[3,1,32,128]{3,2,1,0:T(8,128)S(1)} %get-tuple-element.31), channel_id=1, source_target_pairs={{8,0},{16,8},{24,16},{9,1},{17,9},{25,17},{10,2},{18,10},{26,18},{... | collective-permute-start | bytes 147464 | tf_op jit(solution)/shard_map/ppermute | solution.py:22
  212.5 5.4 %collective-permute-start.12 = (f32[3,1,32,128]{3,2,1,0:T(8,128)S(1)}, f32[3,1,32,128]{3,2,1,0:T(8,128)S(1)}, u32[]{:S(2)}, u32[]{:S(2)}) collective-permute-start(f32[3,1,32,128]{3,2,1,0:T(8,128)S(1)} %get-tuple-element.30), channel_id=1, source_target_pairs={{0,8},{8,16},{16,24},{1,9},{9,17},{17,25},{2,10},{10,18},{18,26},{... | collective-permute-start | bytes 147464 | tf_op jit(solution)/shard_map/ppermute | solution.py:20
  217.9 9.1 %collective-permute-start.15 = (f32[3,34,1,128]{3,2,1,0:T(1,128)S(1)}, f32[3,34,1,128]{3,2,1,0:T(1,128)S(1)}, u32[]{:S(2)}, u32[]{:S(2)}) collective-permute-start(f32[3,34,1,128]{3,2,1,0:T(1,128)S(1)} %get-tuple-element.25), channel_id=1, source_target_pairs={{1,0},{2,1},{3,2},{4,3},{5,4},{6,5},{7,6},{9,8},{10,9},{11,10},{12... | collective-permute-start | bytes 156680 | tf_op jit(solution)/shard_map/ppermute | solution.py:22
  219.2 9.1 %collective-permute-start.14 = (f32[3,34,1,128]{3,2,1,0:T(1,128)S(1)}, f32[3,34,1,128]{3,2,1,0:T(1,128)S(1)}, u32[]{:S(2)}, u32[]{:S(2)}) collective-permute-start(f32[3,34,1,128]{3,2,1,0:T(1,128)S(1)} %get-tuple-element.24), channel_id=1, source_target_pairs={{0,1},{1,2},{2,3},{3,4},{4,5},{5,6},{6,7},{8,9},{9,10},{10,11},{11... | collective-permute-start | bytes 156680 | tf_op jit(solution)/shard_map/ppermute | solution.py:20
  232.3 4.8 %collective-permute-start.21 = (f32[3,1,32,128]{3,2,1,0:T(8,128)S(1)}, f32[3,1,32,128]{3,2,1,0:T(8,128)S(1)}, u32[]{:S(2)}, u32[]{:S(2)}) collective-permute-start(f32[3,1,32,128]{3,2,1,0:T(8,128)S(1)} %get-tuple-element.29), channel_id=1, source_target_pairs={{8,0},{16,8},{24,16},{9,1},{17,9},{25,17},{10,2},{18,10},{26,18},{... | collective-permute-start | bytes 147464 | tf_op jit(solution)/shard_map/ppermute | solution.py:22
  234.2 5.4 %collective-permute-start.20 = (f32[3,1,32,128]{3,2,1,0:T(8,128)S(1)}, f32[3,1,32,128]{3,2,1,0:T(8,128)S(1)}, u32[]{:S(2)}, u32[]{:S(2)}) collective-permute-start(f32[3,1,32,128]{3,2,1,0:T(8,128)S(1)} %get-tuple-element.28), channel_id=1, source_target_pairs={{0,8},{8,16},{16,24},{1,9},{9,17},{17,25},{2,10},{10,18},{18,26},{... | collective-permute-start | bytes 147464 | tf_op jit(solution)/shard_map/ppermute | solution.py:20
  239.7 9.6 %collective-permute-start.23 = (f32[3,34,1,128]{3,2,1,0:T(1,128)S(1)}, f32[3,34,1,128]{3,2,1,0:T(1,128)S(1)}, u32[]{:S(2)}, u32[]{:S(2)}) collective-permute-start(f32[3,34,1,128]{3,2,1,0:T(1,128)S(1)} %get-tuple-element.23), channel_id=1, source_target_pairs={{1,0},{2,1},{3,2},{4,3},{5,4},{6,5},{7,6},{9,8},{10,9},{11,10},{12... | collective-permute-start | bytes 156680 | tf_op jit(solution)/shard_map/ppermute | solution.py:22
  241.0 9.2 %collective-permute-start.22 = (f32[3,34,1,128]{3,2,1,0:T(1,128)S(1)}, f32[3,34,1,128]{3,2,1,0:T(1,128)S(1)}, u32[]{:S(2)}, u32[]{:S(2)}) collective-permute-start(f32[3,34,1,128]{3,2,1,0:T(1,128)S(1)} %get-tuple-element.22), channel_id=1, source_target_pairs={{0,1},{1,2},{2,3},{3,4},{4,5},{5,6},{6,7},{8,9},{9,10},{10,11},{11... | collective-permute-start | bytes 156680 | tf_op jit(solution)/shard_map/ppermute | solution.py:20
  250.2 0.7 copy-start.7
Sparse Core Ops, SparseCore 0:
  14.6 147.2 all-reduce.5
  256.3 138.7 all-reduce.3
where the time goes:
time: 404 us; the launch traced here: 403 us
  waiting for transfers between devices  281 us (70%)
  starting transfers between devices  77.1 us (19%)
  other arithmetic  22.4 us (6%)
  between operations  16.7 us (4%)
  local copies, waits for them, and re-layouts  5.8 us (1%)
    psum x1, waiting for transfers between devices, local(): total = lax.psum(weighted, 'rep')  139 us
    psum x1, waiting for transfers between devices, spread_2(): return lax.psum(jnp.where(mine, x, jnp.zeros_like(x)), axis)  128 us
    ppermute x12, starting transfers between devices, extended(): lax.ppermute(tail, axis, [(i, (i + 1) % count) for i in range(ends)])  52.6 us
    ppermute x12, starting transfers between devices, extended(): lax.ppermute(head, axis, [((i + 1) % count, i) for i in range(ends)])  24.4 us
    ppermute x12, waiting for transfers between devices, extended(): lax.ppermute(tail, axis, [(i, (i + 1) % count) for i in range(ends)])  14 us
  transfers between devices with their start and end apart: 26, of which 7 were waited for; matrix products, arithmetic and copies ran while one was open for 3% of the time, Pallas kernels for 0%

commit v1 on v0

v1 whole, which is shorter than its diff:
```python
import functools

import jax
import jax.numpy as jnp
from jax import lax
from jax.experimental import pallas as pl
from jax.experimental.pallas import tpu as pltpu
from jax.sharding import PartitionSpec as P

F32 = jnp.float32
BF16 = jnp.bfloat16
STEPS = 3
REACH = 3
WIDE = 40
SCALE = 2.0**15
DT = 0.1

LEVEL_HALO = ((0, 0, 3), (1, 0, 2), (0, 1, 2), (1, 1, 1), (0, 2, 1))


def x_index(reps):
    table, at = {}, 0
    for r in range(reps):
        table["f", r] = (at, REACH)
        at += REACH
    for which, level, width in LEVEL_HALO:
        table[which, level] = (at, width)
        at += width
    return table, at


def y_index(reps):
    keys = [("f", r) for r in range(reps)] + [(w, k) for w, k, _ in LEVEL_HALO]
    width = {("f", r): REACH for r in range(reps)}
    width.update({(w, k): n for w, k, n in LEVEL_HALO})
    strips = [(key, d) for key in keys for d in range(1, width[key] + 1)]
    corners = [
        (key, d, e, side)
        for key in keys
        for d in range(1, width[key])
        for e in range(1, width[key] - d + 1)
        for side in (0, 1)
    ]
    return strips, corners


def level_row(lev_ref, which, level, x):
    return lev_ref[x // 2, level, 2 * which + lax.rem(x, 2)]


def pack_kernel(reps, rows, cols, f_ref, lev_ref, up_ref, down_ref, left_ref, right_ref, tile, out):
    xi, _ = x_index(reps)
    strips, corners = y_index(reps)
    keys = []
    for key, _ in strips:
        if key not in keys:
            keys.append(key)
    base = len(strips) * rows
    for side, target in ((0, left_ref), (1, right_ref)):
        lo = 0 if side == 0 else cols - 8
        for key in keys:
            for x in range(rows):
                if key[0] == "f":
                    v = f_ref[key[1], x, lo : lo + 8, :]
                else:
                    v = lev_ref[x // 2, key[1], 2 * key[0] + x % 2, lo : lo + 8, :]
                tile[pl.ds(x * 8, 8), :] = v.astype(F32)
            for n, (k, d) in enumerate(strips):
                if k == key:
                    c = d - 1 if side == 0 else 8 - d
                    target[pl.ds(n * rows, rows), :] = tile[pl.ds(c, rows, stride=8), :].astype(target.dtype)
        out[...] = jnp.zeros_like(out)
        for n, (key, d, e, edge) in enumerate(corners):
            first, width = xi[key]
            row = up_ref[first + width - e, lo : lo + 8, :] if edge == 0 else down_ref[first + e - 1, lo : lo + 8, :]
            c = d - 1 if side == 0 else 8 - d
            out[pl.ds(n, 1), :] = row.astype(F32)[c : c + 1]
        target[pl.ds(base, out.shape[0]), :] = out[...].astype(target.dtype)


def steps_kernel(
    reps, rows, cols,
    coef_ref, f_ref, lev_ref, up_ref, down_ref, left_ref, right_ref,
    adj_ref, sum_ref,
    state, vx, vy, keep, swap, spare,
):
    xi, _ = x_index(reps)
    strips, corners = y_index(reps)
    total = rows + 2 * REACH
    base = len(strips) * rows
    half = 64
    spare_rows = spare.shape[0]

    def fill(target, key, main):
        def body(x, carry):
            target[pl.ds(pl.multiple_of((x + REACH) * WIDE, 8), cols), :] = main(x).astype(F32)
            return carry

        lax.fori_loop(0, rows, body, 0, unroll=4)
        first, width = xi[key]
        for e in range(1, width + 1):
            target[pl.ds((REACH - e) * WIDE, cols), :] = up_ref[first + width - e].astype(F32)
            target[pl.ds((REACH + rows + e - 1) * WIDE, cols), :] = down_ref[first + e - 1].astype(F32)
        for side, source in ((0, left_ref), (1, right_ref)):
            for n, (k, d) in enumerate(strips):
                if k == key:
                    c = WIDE - d if side == 0 else cols + d - 1
                    target[pl.ds(REACH * WIDE + c, rows, stride=WIDE), :] = source[pl.ds(n * rows, rows), :].astype(F32)
            mine = [(n, q) for n, q in enumerate(corners) if q[0] == key]
            for n, (_, d, e, edge) in mine:
                c = WIDE - d if side == 0 else cols + d - 1
                x = REACH - e if edge == 0 else REACH + rows + e - 1
                target[pl.ds(x * WIDE + c, 1), :] = spare[pl.ds(side * (spare_rows // 2) + n, 1), :]

    for side, source in ((0, left_ref), (1, right_ref)):
        spare[pl.ds(side * (spare_rows // 2), spare_rows // 2), :] = source[pl.ds(base, spare_rows // 2), :].astype(F32)

    for r in range(reps):
        fill(state.at[0, r], ("f", r), lambda x, r=r: f_ref[r, x])

    lane = lax.broadcasted_iota(jnp.int32, (WIDE, 128), 1)
    low = lane < half
    for k in range(STEPS):
        now, later = k % 2, (k + 1) % 2
        fill(vx, (0, k), lambda x, k=k: level_row(lev_ref, 0, k, x))
        if k < STEPS - 1:
            fill(keep, (1, k), lambda x, k=k: level_row(lev_ref, 1, k, x))
        else:

            def body3(x, carry):
                keep[pl.ds(pl.multiple_of((x + REACH) * WIDE, 8), cols), :] = level_row(lev_ref, 1, STEPS - 1, x).astype(F32)
                return carry

            lax.fori_loop(0, rows, body3, 0, unroll=4)

        def coefficients(x, carry):
            at = pl.ds(pl.multiple_of(x * WIDE, 8), WIDE)
            v = vx[at, :] * (0.5 * DT / SCALE)
            t = keep[at, :]
            o = pltpu.roll(v, half, axis=1)
            vx[at, :] = jnp.where(low, v, o)
            vy[at, :] = jnp.where(low, o, v)
            keep[at, :] = jnp.where(t > 0.0, (1.0 - 4.0 * DT) - DT * t, 4.0)
            swap[at, :] = DT * pltpu.roll(t, half, axis=1)
            return carry

        lax.fori_loop(k, total - k, coefficients, 0)

        def row(x, carry):
            at = pl.ds(pl.multiple_of(x * WIDE, 8), WIDE)
            above = pl.ds(pl.multiple_of((x - 1) * WIDE, 8), WIDE)
            below = pl.ds(pl.multiple_of((x + 1) * WIDE, 8), WIDE)
            a = DT + vx[above, :]
            b = DT - vx[below, :]
            y = vy[at, :]
            c, d = DT + y, DT - y
            centre = keep[at, :]
            other = swap[at, :]
            ocean = centre < 1.0
            weighted = None
            for r in range(reps):
                s = state[now, r, at, :]
                new = (
                    a * state[now, r, above, :]
                    + b * state[now, r, below, :]
                    + pltpu.roll(c * s, 1, axis=0)
                    + pltpu.roll(d * s, WIDE - 1, axis=0)
                    + centre * s
                    + other * pltpu.roll(s, half, axis=1)
                )
                new = jnp.where(ocean, new, 0.0)
                if k < STEPS - 1:
                    state[later, r, at, :] = new
                else:
                    own = new[:cols]
                    adj_ref[r, x - REACH] = own
                    part = coef_ref[r] * own
                    weighted = part if weighted is None else weighted + part
            if k == STEPS - 1:
                sum_ref[x - REACH] = weighted
            return carry

        lax.fori_loop(k + 1, total - k - 1, row, 0)


def shift(x, axis, by):
    n = lax.axis_size(axis)
    if by > 0:
        return lax.ppermute(x, axis, [(i, i + 1) for i in range(n - 1)])
    return lax.ppermute(x, axis, [(i + 1, i) for i in range(n - 1)])


def local(velocity, tracers, forcing, coefficients, land_mask, step_levels):
    groups = lax.axis_size("rep")
    reps, rows, cols, lanes = forcing.shape
    own = rows // groups
    ocean = (land_mask > 0)[:, :, None]
    tracer = jnp.where(ocean, tracers[0], jnp.zeros_like(tracers[0]))
    speed = velocity[0] * BF16(SCALE)
    mine = jnp.concatenate([speed.reshape(groups, own, cols, lanes), tracer.reshape(groups, own, cols, lanes)], axis=1)
    slices = lax.all_to_all(mine, "rep", 0, 0, tiled=True)
    picked = jnp.stack([lax.dynamic_index_in_dim(slices, step_levels[k], 0, False) for k in range(STEPS)])
    lev = lax.all_gather(picked.astype(jnp.float16), "rep", axis=0, tiled=False)
    lev = lax.optimization_barrier(lev).astype(BF16)

    def edge(rows_of, source):
        return [source[x // own, k, which * own + x % own] for which, k, x in rows_of]

    last, first = [], []
    for which, k, width in LEVEL_HALO:
        last += [(which, k, rows - width + i) for i in range(width)]
        first += [(which, k, i) for i in range(width)]
    to_down = jnp.concatenate([forcing[:, rows - REACH :].reshape(-1, cols, lanes), jnp.stack(edge(last, lev))])
    to_up = jnp.concatenate([forcing[:, :REACH].reshape(-1, cols, lanes), jnp.stack(edge(first, lev))])
    up = shift(to_down, "gx", 1)
    down = shift(to_up, "gx", -1)

    strips, corners = y_index(reps)
    extra = -(-len(corners) // 16) * 16
    length = len(strips) * rows + extra
    payload = jax.ShapeDtypeStruct((length, lanes), BF16)
    to_left, to_right = pl.pallas_call(
        functools.partial(pack_kernel, reps, rows, cols),
        out_shape=(payload, payload),
        scratch_shapes=[pltpu.VMEM((rows * 8, lanes), F32), pltpu.VMEM((extra, lanes), F32)],
        name="pack",
    )(forcing, lev, up, down)
    right = shift(to_left, "gy", -1)
    left = shift(to_right, "gy", 1)

    vm = pl.BlockSpec(memory_space=pltpu.VMEM)
    size = (rows + 2 * REACH) * WIDE
    adjoints, weighted = pl.pallas_call(
        functools.partial(steps_kernel, reps, rows, cols),
        out_shape=(
            jax.ShapeDtypeStruct((reps, rows, cols, lanes), F32),
            jax.ShapeDtypeStruct((rows, cols, lanes), F32),
        ),
        in_specs=[pl.BlockSpec(memory_space=pltpu.SMEM)] + [vm] * 6,
        out_specs=(vm, vm),
        scratch_shapes=[pltpu.VMEM((2, reps, size, lanes), F32)]
        + [pltpu.VMEM((size, lanes), F32)] * 4
        + [pltpu.VMEM((2 * extra, lanes), F32)],
        name="steps",
    )(coefficients, forcing, lev, up, down, left, right)

    parts = lax.all_to_all(weighted.reshape(groups, own, cols, lanes), "rep", 0, 0, tiled=True)
    return jnp.sum(parts, axis=0), adjoints


def solution(mesh):
    placed = (
        P("rep", "gx", "gy", None),
        P("rep", "gx", "gy", None),
        P("rep", "gx", "gy", None),
        P("rep"),
        P("gx", "gy"),
        P(),
    )
    return jax.shard_map(
        local,
        mesh=mesh,
        in_specs=placed,
        out_specs=(P(("gx", "rep"), "gy", None), P("rep", "gx", "gy", None)),
        check_vma=False,
    )
```

time: 404 us -> 173 us (0.43)
  the two profiles are of different devices: /device:TPU:2 before, /device:TPU:32 now
where the time goes in v1:
time: 173 us; the launch traced here: 172 us
  blocking collectives  75.7 us (44%)
  waiting for transfers between devices  30.5 us (18%)
  starting transfers between devices  25.8 us (15%)
  Pallas kernels  25.5 us (15%)
  between operations  6.66 us (4%)
  other arithmetic  4.71 us (3%)
  local copies, waits for them, and re-layouts  3.08 us (2%)
    all_to_all x1, blocking collectives, local(): lax.all_to_all(weighted.reshape(groups, own, cols, lanes), 'rep', 0, 0, t...  38.2 us
    all_gather x1, blocking collectives, local(): lev = lax.all_gather(picked.astype(jnp.float16), 'rep', axis=0, tiled=False)  37.5 us
    pallas_call x1, Pallas kernels, local(): pl.pallas_call(functools.partial(steps_kernel, reps, rows, cols), out_sha...  22.9 us
    all_to_all x1, waiting for transfers between devices, local(): slices = lax.all_to_all(mine, 'rep', 0, 0, tiled=True)  21 us
    all_to_all x1, starting transfers between devices, local(): slices = lax.all_to_all(mine, 'rep', 0, 0, tiled=True)  15.2 us
    ppermute x2, starting transfers between devices, shift(): return lax.ppermute(x, axis, [(i, i + 1) for i in range(n - 1)])  7.96 us
    ppermute x2, waiting for transfers between devices, shift(): return lax.ppermute(x, axis, [(i + 1, i) for i in range(n - 1)])  6.08 us
  transfers between devices with their start and end apart: 5, of which 4 were waited for; matrix products, arithmetic and copies ran while one was open for 1% of the time, Pallas kernels for 0%

profile of v1, /device:TPU:32, one launch (start us, length us, event | category | flops | bytes accessed | tf_op | source)
XLA Modules:
  0.0 171.9 jit_solution(879358140204568485)
XLA Ops:
  0.6 0.7 broadcast_compare_fusion
  1.4 0.0 copy-start.5
  1.4 1.0 broadcast_multiply_fusion
  2.4 1.2 broadcast_select_fusion
  3.5 0.8 pad_maximum_fusion
  4.4 15.2 %all-to-all-start = ((bf16[16,4,32,128]{3,2,1,0:T(8,128)(2,1)}), bf16[16,4,32,128]{3,2,1,0:T(8,128)(2,1)S(1)}, u32[]{:S(2)}, u32[]{:S(2)}) async-start(bf16[16,4,32,128]{3,2,1,0:T(8,128)(2,1)} %pad_maximum_fusion), calls=%async_computation | async-start | bytes 1048576 | tf_op jit(solution)/shard_map/all_to_all | solution.py:201
  19.6 0.0 copy-done.5
  19.6 0.7 fusion.1
  26.1 0.9 fusion
  27.1 21.0 %all-to-all-done = bf16[16,4,32,128]{3,2,1,0:T(8,128)(2,1)S(1)} async-done(((bf16[16,4,32,128]{3,2,1,0:T(8,128)(2,1)}), bf16[16,4,32,128]{3,2,1,0:T(8,128)(2,1)S(1)}, u32[]{:S(2)}, u32[]{:S(2)}) %all-to-all-start) | async-done | bytes 524320 | tf_op jit(solution)/shard_map/all_to_all | solution.py:201
  48.1 37.5 %all-gather.1 = f16[16,3,4,32,128]{4,3,2,1,0:T(8,128)(2,1)S(1)} all-gather(f16[1,3,4,32,128]{4,3,2,1,0:T(8,128)(2,1)S(1)} %maximum_convert_fusion), channel_id=1, replica_groups=mesh['rep'=16,'gx'=4,'gy'=8] {'rep'}, dimensions={0}, use_global_device_ids=true | all-gather | bytes 1671168 | tf_op jit(solution)/shard_map/all_gather | solution.py:203
  85.6 0.3 convert_element_type.14.lev_ref
  86.0 0.0 copy-start
  86.1 1.3 collective-permute-start.1
  87.4 3.0 %collective-permute-start = (bf16[18,32,128]{2,1,0:T(8,128)(2,1)S(1)}, bf16[18,32,128]{2,1,0:T(8,128)(2,1)S(1)}, u32[]{:S(2)}, u32[]{:S(2)}) collective-permute-start(bf16[18,32,128]{2,1,0:T(8,128)(2,1)S(1)} %get-tuple-element.11), channel_id=1, source_target_pairs={{0,8},{8,16},{16,24},{1,9},{9,17},{17,25},{2,10},{10,18},{18,26},{... | collective-permute-start | bytes 442376 | tf_op jit(solution)/shard_map/ppermute | solution.py:189
  90.4 0.0 collective-permute-done.1.down_ref
  90.4 0.0 copy-start.1
  90.5 1.0 collective-permute-done.up_ref
  91.4 0.0 copy-done
  91.4 0.0 copy-done.1
  91.4 0.0 copy-start.2
  91.4 0.7 copy-done.2
  92.1 2.6 %pack.1 = (bf16[608,128]{1,0:T(8,128)(2,1)}, bf16[608,128]{1,0:T(8,128)(2,1)}) custom-call(bf16[3,32,32,128]{3,2,1,0:T(8,128)(2,1)} %f_ref.3, bf16[16,3,4,32,128]{4,3,2,1,0:T(8,128)(2,1)} %copy-done, bf16[18,32,128]{2,1,0:T(8,128)(2,1)} %copy-done.2, bf16[18,32,128]{2,1,0:T(8,128)(2,1)} %copy-done.1), custom_call_target="tpu_custom_call" | custom-call | tf_op jit(solution)/shard_map/pack/pallas_call | solution.py:222
  94.7 4.9 %collective-permute-start.2 = (bf16[608,128]{1,0:T(8,128)(2,1)}, bf16[608,128]{1,0:T(8,128)(2,1)S(1)}, u32[]{:S(2)}, u32[]{:S(2)}) collective-permute-start(bf16[608,128]{1,0:T(8,128)(2,1)} %get-tuple-element.6), channel_id=1, source_target_pairs={{0,1},{1,2},{2,3},{3,4},{4,5},{5,6},{6,7},{8,9},{9,10},{10,11},{11... | collective-permute-start | bytes 466952 | tf_op jit(solution)/shard_map/ppermute | solution.py:189
  99.6 1.3 collective-permute-start.3
  100.9 2.5 %collective-permute-done.2.left_ref = bf16[608,128]{1,0:T(8,128)(2,1)S(1)} collective-permute-done((bf16[608,128]{1,0:T(8,128)(2,1)}, bf16[608,128]{1,0:T(8,128)(2,1)S(1)}, u32[]{:S(2)}, u32[]{:S(2)}) %collective-permute-start.2) | collective-permute-done | bytes 155680 | tf_op jit(solution)/shard_map/ppermute | solution.py:189
  103.4 0.0 copy-start.3
  103.4 6.1 %collective-permute-done.3.right_ref = bf16[608,128]{1,0:T(8,128)(2,1)S(1)} collective-permute-done((bf16[608,128]{1,0:T(8,128)(2,1)}, bf16[608,128]{1,0:T(8,128)(2,1)S(1)}, u32[]{:S(2)}, u32[]{:S(2)}) %collective-permute-start.3) | collective-permute-done | bytes 155680 | tf_op jit(solution)/shard_map/ppermute | solution.py:190
  109.5 0.0 copy-done.3
  109.5 0.0 copy-start.4
  109.5 0.7 copy-done.4
  110.1 22.9 %steps.1 = (f32[3,32,32,128]{3,2,1,0:T(8,128)}, f32[32,32,128]{2,1,0:T(8,128)}) custom-call(f32[3]{0:T(128)} %coef_ref.1, bf16[3,32,32,128]{3,2,1,0:T(8,128)(2,1)} %f_ref.3, bf16[16,3,4,32,128]{4,3,2,1,0:T(8,128)(2,1)} %copy-done, bf16[18,32,128]{2,1,0:T(8,128)(2,1)} %copy-done.2, bf16[18,32,128]{2,1,0:T(8,128)(2,1)} %copy-done.1, ...), custom_call_target="tpu_custom_call" | custom-call | tf_op jit(solution)/shard_map/steps/pallas_call | solution.py:233
  133.0 38.2 %all_to_all.10 = f32[16,2,32,128]{3,2,1,0:T(8,128)S(1)} all-to-all(f32[16,2,32,128]{3,2,1,0:T(8,128)} %bitcast.87), channel_id=1, replica_groups=mesh['rep'=16,'gx'=4,'gy'=8] {'rep'}, dimensions={0} | all-to-all | bytes 1048576 | tf_op jit(solution)/shard_map/all_to_all | solution.py:247
  171.3 0.6 reduce_sum.9
  (13 shorter events, 0.2 us)
Async XLA Ops:
  1.4 18.2 %copy-start.5 = (s32[3]{0:T(128)S(1)}, s32[3]{0:T(128)}, u32[]{:S(2)}) copy-start(s32[3]{0:T(128)} %param.11) | copy-start | bytes 40
  4.4 43.7 %all-to-all-start = ((bf16[16,4,32,128]{3,2,1,0:T(8,128)(2,1)}), bf16[16,4,32,128]{3,2,1,0:T(8,128)(2,1)S(1)}, u32[]{:S(2)}, u32[]{:S(2)}) async-start(bf16[16,4,32,128]{3,2,1,0:T(8,128)(2,1)} %pad_maximum_fusion), calls=%async_computation | async-start | bytes 1048576 | tf_op jit(solution)/shard_map/all_to_all | solution.py:201
  86.0 5.5 %copy-start = (bf16[16,3,4,32,128]{4,3,2,1,0:T(8,128)(2,1)}, bf16[16,3,4,32,128]{4,3,2,1,0:T(8,128)(2,1)S(1)}, u32[]{:S(2)}) copy-start(bf16[16,3,4,32,128]{4,3,2,1,0:T(8,128)(2,1)S(1)} %convert_element_type.14.lev_ref) | copy-start | bytes 4718596
  86.1 4.3 %collective-permute-start.1 = (bf16[18,32,128]{2,1,0:T(8,128)(2,1)S(1)}, bf16[18,32,128]{2,1,0:T(8,128)(2,1)S(1)}, u32[]{:S(2)}, u32[]{:S(2)}) collective-permute-start(bf16[18,32,128]{2,1,0:T(8,128)(2,1)S(1)} %get-tuple-element.10), channel_id=1, source_target_pairs={{8,0},{16,8},{24,16},{9,1},{17,9},{25,17},{10,2},{18,10},{26,18},{... | collective-permute-start | bytes 442376 | tf_op jit(solution)/shard_map/ppermute | solution.py:190
  87.4 4.0 %collective-permute-start = (bf16[18,32,128]{2,1,0:T(8,128)(2,1)S(1)}, bf16[18,32,128]{2,1,0:T(8,128)(2,1)S(1)}, u32[]{:S(2)}, u32[]{:S(2)}) collective-permute-start(bf16[18,32,128]{2,1,0:T(8,128)(2,1)S(1)} %get-tuple-element.11), channel_id=1, source_target_pairs={{0,8},{8,16},{16,24},{1,9},{9,17},{17,25},{2,10},{10,18},{18,26},{... | collective-permute-start | bytes 442376 | tf_op jit(solution)/shard_map/ppermute | solution.py:189
  90.4 1.0 copy-start.1
  91.4 0.7 copy-start.2
  94.7 8.7 %collective-permute-start.2 = (bf16[608,128]{1,0:T(8,128)(2,1)}, bf16[608,128]{1,0:T(8,128)(2,1)S(1)}, u32[]{:S(2)}, u32[]{:S(2)}) collective-permute-start(bf16[608,128]{1,0:T(8,128)(2,1)} %get-tuple-element.6), channel_id=1, source_target_pairs={{0,1},{1,2},{2,3},{3,4},{4,5},{5,6},{6,7},{8,9},{9,10},{10,11},{11... | collective-permute-start | bytes 466952 | tf_op jit(solution)/shard_map/ppermute | solution.py:189
  99.6 9.8 %collective-permute-start.3 = (bf16[608,128]{1,0:T(8,128)(2,1)}, bf16[608,128]{1,0:T(8,128)(2,1)S(1)}, u32[]{:S(2)}, u32[]{:S(2)}) collective-permute-start(bf16[608,128]{1,0:T(8,128)(2,1)} %get-tuple-element.7), channel_id=1, source_target_pairs={{1,0},{2,1},{3,2},{4,3},{5,4},{6,5},{7,6},{9,8},{10,9},{11,10},{12... | collective-permute-start | bytes 466952 | tf_op jit(solution)/shard_map/ppermute | solution.py:190
  103.4 6.1 %copy-start.3 = (bf16[608,128]{1,0:T(8,128)(2,1)}, bf16[608,128]{1,0:T(8,128)(2,1)S(1)}, u32[]{:S(2)}) copy-start(bf16[608,128]{1,0:T(8,128)(2,1)S(1)} %collective-permute-done.2.left_ref) | copy-start | bytes 466948
  109.5 0.7 copy-start.4

commit v2 on v1

v2 whole, which is shorter than its diff:
```python
import functools

import jax
import jax.numpy as jnp
from jax import lax
from jax.experimental import pallas as pl
from jax.experimental.pallas import tpu as pltpu
from jax.sharding import PartitionSpec as P

F32 = jnp.float32
BF16 = jnp.bfloat16
STEPS = 3
REACH = 3
WIDE = 40
SCALE = 2.0**15
DT = 0.1

LEVEL_HALO = ((0, 0, 3), (1, 0, 2), (0, 1, 2), (1, 1, 1), (0, 2, 1))


def x_index(reps):
    table, at = {}, 0
    for r in range(reps):
        table["f", r] = (at, REACH)
        at += REACH
    for which, level, width in LEVEL_HALO:
        table[which, level] = (at, width)
        at += width
    return table, at


def y_index(reps):
    keys = [("f", r) for r in range(reps)] + [(w, k) for w, k, _ in LEVEL_HALO]
    width = {("f", r): REACH for r in range(reps)}
    width.update({(w, k): n for w, k, n in LEVEL_HALO})
    strips = [(key, d) for key in keys for d in range(1, width[key] + 1)]
    corners = [
        (key, d, e, side)
        for key in keys
        for d in range(1, width[key])
        for e in range(1, width[key] - d + 1)
        for side in (0, 1)
    ]
    return strips, corners


def pack_kernel(reps, rows, cols, f_ref, lev_ref, up_ref, down_ref, left_ref, right_ref, tile, out):
    xi, _ = x_index(reps)
    strips, corners = y_index(reps)
    keys = []
    for key, _ in strips:
        if key not in keys:
            keys.append(key)
    base = len(strips) * rows
    for side, target in ((0, left_ref), (1, right_ref)):
        lo = 0 if side == 0 else cols - 8
        for key in keys:
            for x in range(rows):
                if key[0] == "f":
                    v = f_ref[key[1], x, lo : lo + 8, :]
                else:
                    v = lev_ref[x // 2, key[1], 2 * key[0] + x % 2, lo : lo + 8, :]
                tile[pl.ds(x * 8, 8), :] = v.astype(F32)
            for n, (k, d) in enumerate(strips):
                if k == key:
                    c = d - 1 if side == 0 else 8 - d
                    target[pl.ds(n * rows, rows), :] = tile[pl.ds(c, rows, stride=8), :].astype(target.dtype)
        out[...] = jnp.zeros_like(out)
        for n, (key, d, e, edge) in enumerate(corners):
            first, width = xi[key]
            row = up_ref[first + width - e, lo : lo + 8, :] if edge == 0 else down_ref[first + e - 1, lo : lo + 8, :]
            c = d - 1 if side == 0 else 8 - d
            out[pl.ds(n, 1), :] = row.astype(F32)[c : c + 1]
        target[pl.ds(base, out.shape[0]), :] = out[...].astype(target.dtype)


def own_kernel(groups, own, v_hbm, t_hbm, mask_hbm, out, v_ref, t_ref, mask_ref, sems):
    copies = [
        pltpu.make_async_copy(source, target, sems.at[n])
        for n, (source, target) in enumerate(((mask_hbm, mask_ref), (v_hbm, v_ref), (t_hbm, t_ref)))
    ]
    for copy in copies:
        copy.start()
    copies[0].wait()
    ocean = jnp.transpose(mask_ref[...].astype(F32))
    copies[1].wait()
    for x in range(groups * own):
        out[x // own, x % own] = v_ref[0, x] * BF16(SCALE)
    copies[2].wait()
    for x in range(groups * own):
        t = t_ref[0, x].astype(F32)
        out[x // own, own + x % own] = jnp.where(ocean[:, x : x + 1] > 0.0, t, 0.0).astype(BF16)


def pick_kernel(levels_ref, slices_ref, out):
    for k in range(STEPS):
        out[k] = slices_ref[levels_ref[k]]


def steps_kernel(
    reps, rows, cols,
    coef_ref, f_ref, lev_ref, up_ref, down_ref, left_ref, right_ref,
    adj_hbm, sum_ref,
    state, vx, vy, keep, swap, spare, adj_ref, sems,
):
    xi, _ = x_index(reps)
    strips, corners = y_index(reps)
    total = rows + 2 * REACH
    base = len(strips) * rows
    half = 64
    extra = spare.shape[0] // 2

    def put_state(r):
        def put(at, v):
            state[0, r, at, :] = v

        return put

    def put_speed(at, v):
        v = v * (0.5 * DT / SCALE)
        o = pltpu.roll(v, half, axis=1)
        is_low = lax.broadcasted_iota(jnp.int32, v.shape, 1) < half
        vx[at, :] = jnp.where(is_low, v, o)
        vy[at, :] = jnp.where(is_low, o, v)

    def put_tracer(at, t):
        keep[at, :] = jnp.where(t > 0.0, (1.0 - 4.0 * DT) - DT * t, 4.0)
        swap[at, :] = DT * pltpu.roll(t, half, axis=1)

    def fill(put, key):
        if key in xi:
            first, width = xi[key]
            for e in range(1, width + 1):
                put(pl.ds((REACH - e + 1) * WIDE, cols), up_ref[first + width - e].astype(F32))
                put(pl.ds((REACH + rows + e) * WIDE, cols), down_ref[first + e - 1].astype(F32))
        for side, source in ((0, left_ref), (1, right_ref)):
            for n, (k, d) in enumerate(strips):
                if k == key:
                    c = -d if side == 0 else cols + d - 1
                    at = pl.ds((REACH + 1) * WIDE + c, rows, stride=WIDE)
                    put(at, source[pl.ds(n * rows, rows), :].astype(F32))
            for n, (k, d, e, edge) in enumerate(corners):
                if k == key:
                    c = -d if side == 0 else cols + d - 1
                    x = REACH - e if edge == 0 else REACH + rows + e - 1
                    put(pl.ds((x + 1) * WIDE + c, 1), spare[pl.ds(side * extra + n, 1), :])

    spare[pl.ds(0, extra), :] = left_ref[pl.ds(base, extra), :].astype(F32)
    spare[pl.ds(extra, extra), :] = right_ref[pl.ds(base, extra), :].astype(F32)

    def forcing_row(x, carry):
        at = pl.ds(pl.multiple_of((x + REACH + 1) * WIDE, 8), cols)
        for r in range(reps):
            state[0, r, at, :] = f_ref[r, x].astype(F32)
        return carry

    lax.fori_loop(0, rows, forcing_row, 0, unroll=4)
    for r in range(reps):
        fill(put_state(r), ("f", r))

    for k in range(STEPS):
        now, later = k % 2, (k + 1) % 2

        def level_rows(g, carry, k=k):
            own = lev_ref.shape[2] // 2
            for i in range(own):
                at = pl.ds(pl.multiple_of((g * own + i + REACH + 1) * WIDE, 8), cols)
                put_speed(at, lev_ref[g, k, i].astype(F32))
                put_tracer(at, lev_ref[g, k, own + i].astype(F32))
            return carry

        lax.fori_loop(0, lev_ref.shape[0], level_rows, 0)
        fill(put_speed, (0, k))
        fill(put_tracer, (1, k))

        def row(x, carry, k=k, now=now, later=later):
            start = pl.multiple_of(x * WIDE, 8)
            for j in range(0, cols if k == STEPS - 1 else WIDE, 8):
                at = pl.ds(start + j, 8)
                above, below = pl.ds(start + j - WIDE, 8), pl.ds(start + j + WIDE, 8)
                before, after = pl.ds(start + j - 1, 8), pl.ds(start + j + 1, 8)
                a = DT + vx[above, :]
                b = DT - vx[below, :]
                c = DT + vy[before, :]
                d = DT - vy[after, :]
                centre = keep[at, :]
                other = swap[at, :]
                ocean = centre < 1.0
                weighted = None
                for r in range(reps):
                    s = state[now, r, at, :]
                    new = (
                        (a * state[now, r, above, :] + b * state[now, r, below, :])
                        + (c * state[now, r, before, :] + d * state[now, r, after, :])
                        + (centre * s + other * pltpu.roll(s, half, axis=1))
                    )
                    new = jnp.where(ocean, new, 0.0)
                    if k < STEPS - 1:
                        state[later, r, at, :] = new
                    else:
                        adj_ref[r, x - REACH - 1, pl.ds(j, 8)] = new
                        part = coef_ref[r] * new
                        weighted = part if weighted is None else weighted + part
                if k == STEPS - 1:
                    sum_ref[x - REACH - 1, pl.ds(j, 8)] = weighted
            return carry

        if k < STEPS - 1:
            lax.fori_loop(k + 1, total - k, row, 0)

    stretch = rows // sems.shape[0]

    def out_copy(g):
        at = pl.ds(g * stretch, stretch)
        return pltpu.make_async_copy(adj_ref.at[:, at], adj_hbm.at[:, at], sems.at[g])

    def some_rows(g, carry):
        lax.fori_loop(REACH + 1 + g * stretch, REACH + 1 + (g + 1) * stretch, row, 0)
        out_copy(g).start()
        return carry

    lax.fori_loop(0, sems.shape[0], some_rows, 0)
    for g in range(sems.shape[0]):
        out_copy(g).wait()


def shift(x, axis, by):
    n = lax.axis_size(axis)
    if by > 0:
        return lax.ppermute(x, axis, [(i, i + 1) for i in range(n - 1)])
    return lax.ppermute(x, axis, [(i + 1, i) for i in range(n - 1)])


def local(velocity, tracers, forcing, coefficients, land_mask, step_levels):
    groups = lax.axis_size("rep")
    reps, rows, cols, lanes = forcing.shape
    own = rows // groups
    hbm = pl.BlockSpec(memory_space=pltpu.HBM)
    mine = pl.pallas_call(
        functools.partial(own_kernel, groups, own),
        out_shape=jax.ShapeDtypeStruct((groups, 2 * own, cols, lanes), BF16),
        in_specs=[hbm] * 3,
        scratch_shapes=[
            pltpu.VMEM(velocity.shape, BF16),
            pltpu.VMEM(tracers.shape, BF16),
            pltpu.VMEM(land_mask.shape, land_mask.dtype),
            pltpu.SemaphoreType.DMA((3,)),
        ],
        compiler_params=pltpu.CompilerParams(vmem_limit_bytes=8 * 2**20),
        name="own",
    )(velocity, tracers, land_mask)
    slices = lax.all_to_all(mine, "rep", 0, 0, tiled=True)
    slices, forcing, step_levels = lax.optimization_barrier((slices, forcing, step_levels))
    picked = pl.pallas_call(
        pick_kernel,
        out_shape=jax.ShapeDtypeStruct((STEPS, 2 * own, cols, lanes), BF16),
        in_specs=[pl.BlockSpec(memory_space=pltpu.SMEM), pl.BlockSpec(memory_space=pltpu.VMEM)],
        compiler_params=pltpu.CompilerParams(vmem_limit_bytes=8 * 2**20),
        name="pick",
    )(step_levels, slices)
    lev = lax.all_gather(picked.astype(jnp.float16), "rep", axis=0, tiled=False)
    lev = lax.optimization_barrier(lev).astype(BF16)

    def edge(rows_of, source):
        return [source[x // own, k, which * own + x % own] for which, k, x in rows_of]

    last, first = [], []
    for which, k, width in LEVEL_HALO:
        last += [(which, k, rows - width + i) for i in range(width)]
        first += [(which, k, i) for i in range(width)]
    to_down = jnp.concatenate([forcing[:, rows - REACH :].reshape(-1, cols, lanes), jnp.stack(edge(last, lev))])
    to_up = jnp.concatenate([forcing[:, :REACH].reshape(-1, cols, lanes), jnp.stack(edge(first, lev))])
    up = shift(to_down, "gx", 1)
    down = shift(to_up, "gx", -1)

    strips, corners = y_index(reps)
    extra = -(-len(corners) // 16) * 16
    length = len(strips) * rows + extra
    payload = jax.ShapeDtypeStruct((length, lanes), BF16)
    to_left, to_right = pl.pallas_call(
        functools.partial(pack_kernel, reps, rows, cols),
        out_shape=(payload, payload),
        scratch_shapes=[pltpu.VMEM((rows * 8, lanes), F32), pltpu.VMEM((extra, lanes), F32)],
        compiler_params=pltpu.CompilerParams(vmem_limit_bytes=8 * 2**20),
        name="pack",
    )(forcing, lev, up, down)
    right = shift(to_left, "gy", -1)
    left = shift(to_right, "gy", 1)

    vm = pl.BlockSpec(memory_space=pltpu.VMEM)
    size = (rows + 2 * REACH + 2) * WIDE
    adjoints, weighted = pl.pallas_call(
        functools.partial(steps_kernel, reps, rows, cols),
        out_shape=(
            jax.ShapeDtypeStruct((reps, rows, cols, lanes), F32),
            jax.ShapeDtypeStruct((rows, cols, lanes), F32),
        ),
        in_specs=[pl.BlockSpec(memory_space=pltpu.SMEM)] + [vm] * 6,
        out_specs=(hbm, vm),
        scratch_shapes=[pltpu.VMEM((2, reps, size, lanes), F32)]
        + [pltpu.VMEM((size, lanes), F32)] * 4
        + [pltpu.VMEM((2 * extra, lanes), F32), pltpu.VMEM((reps, rows, cols, lanes), F32), pltpu.SemaphoreType.DMA((4,))],
        compiler_params=pltpu.CompilerParams(vmem_limit_bytes=24 * 2**20),
        name="steps",
    )(coefficients, forcing, lev, up, down, left, right)

    parts = lax.all_to_all(weighted.reshape(groups, own, cols, lanes), "rep", 0, 0, tiled=True)
    return jnp.sum(parts, axis=0), adjoints


def solution(mesh):
    placed = (
        P("rep", "gx", "gy", None),
        P("rep", "gx", "gy", None),
        P("rep", "gx", "gy", None),
        P("rep"),
        P("gx", "gy"),
        P(),
    )
    return jax.shard_map(
        local,
        mesh=mesh,
        in_specs=placed,
        out_specs=(P(("gx", "rep"), "gy", None), P("rep", "gx", "gy", None)),
        check_vma=False,
    )
```

time: 173 us -> 160 us (0.925)
  blocking collectives: 75.7 us -> 119 us
  waiting for transfers between devices: 30.5 us -> 9.31 us
  starting transfers between devices: 25.8 us -> 10.6 us
  Pallas kernels: 25.5 us -> 16.2 us
  between operations: 6.66 us -> 0.8 us
  other arithmetic: 4.71 us -> 1 us
    all_to_all x0 -> x1, blocking collectives: none -> 43.5 us  [local(): slices = lax.all_to_all(mine, 'rep', 0, 0, tiled=True)]
    all_to_all x1 -> x0, waiting for transfers between devices: 21 us -> none  [local(): slices = lax.all_to_all(mine, 'rep', 0, 0, tiled=True)]
    all_to_all x1 -> x0, starting transfers between devices: 15.2 us -> none  [local(): slices = lax.all_to_all(mine, 'rep', 0, 0, tiled=True)]
    pallas_call x1, Pallas kernels: 22.9 us -> 14.9 us  [local(): pl.pallas_call(functools.partial(steps_kernel, reps, rows, cols), out_sha...]
    pallas_call x1, Pallas kernels: 2.59 us -> 0.27 us  [local(): pl.pallas_call(functools.partial(pack_kernel, reps, rows, cols), out_shap...]
  transfers between devices with their start and end apart: 5 -> 4, of which waited for: 4 -> 3; matrix products, arithmetic and copies ran while one was open for 1% -> 0% of each run, Pallas kernels for 0% -> 0%
where the time goes in v2:
time: 160 us
  blocking collectives  119 us (74%)
  Pallas kernels  16.2 us (10%)
  starting transfers between devices  10.6 us (7%)
  waiting for transfers between devices  9.31 us (6%)
  local copies, waits for them, and re-layouts  2.81 us (2%)
    all_to_all x1, blocking collectives, local(): slices = lax.all_to_all(mine, 'rep', 0, 0, tiled=True)  43.5 us
    all_to_all x1, blocking collectives, local(): lax.all_to_all(weighted.reshape(groups, own, cols, lanes), 'rep', 0, 0, t...  38 us
    all_gather x1, blocking collectives, local(): lev = lax.all_gather(picked.astype(jnp.float16), 'rep', axis=0, tiled=False)  37.5 us
    pallas_call x1, Pallas kernels, local(): pl.pallas_call(functools.partial(steps_kernel, reps, rows, cols), out_sha...  14.9 us
    ppermute x2, starting transfers between devices, shift(): return lax.ppermute(x, axis, [(i, i + 1) for i in range(n - 1)])  7.98 us
    ppermute x2, waiting for transfers between devices, shift(): return lax.ppermute(x, axis, [(i + 1, i) for i in range(n - 1)])  6.19 us
  transfers between devices with their start and end apart: 4, of which 3 were waited for; matrix products, arithmetic and copies ran while one was open for 0% of the time, Pallas kernels for 0%

profile of v2, /device:TPU:32, one launch (start us, length us, event | category | flops | bytes accessed | tf_op | source)
XLA Modules:
  0.0 159.7 jit_solution(10439075850268235380)
XLA Ops:
  0.6 0.0 copy-start
  0.6 0.0 copy-start.1
  0.7 1.0 copy-done.1
  1.7 0.0 copy-start.2
  1.7 0.9 copy-done.2
  2.6 0.0 copy-start.3
  2.6 0.7 copy-done.3
  3.3 0.0 copy-start.5
  3.3 0.5 own.1
  3.8 43.5 %all_to_all.10.slices_ref = bf16[16,4,32,128]{3,2,1,0:T(8,128)(2,1)S(1)} all-to-all(bf16[16,4,32,128]{3,2,1,0:T(8,128)(2,1)S(1)} %own.1), channel_id=1, replica_groups=mesh['rep'=16,'gx'=4,'gy'=8] {'rep'}, dimensions={0} | all-to-all | bytes 1048576 | tf_op jit(solution)/shard_map/all_to_all | solution.py:252
  47.3 0.0 copy-done.5
  47.3 0.6 pick.1
  47.9 0.0 copy-done
  47.9 37.5 %all-gather.2 = f16[48,4,32,128]{3,2,1,0:T(8,128)(2,1)S(1)} all-gather(f16[3,4,32,128]{3,2,1,0:T(8,128)(2,1)S(1)} %convert_element_type.6), channel_id=2, replica_groups=mesh['rep'=16,'gx'=4,'gy'=8] {'rep'}, dimensions={0}, use_global_device_ids=true | all-gather | bytes 1671168 | tf_op jit(solution)/shard_map/all_gather | solution.py:261
  85.4 0.3 convert_element_type.7.lev_ref
  85.8 0.0 copy-start.4
  85.9 1.3 collective-permute-start.1
  87.2 3.0 %collective-permute-start = (bf16[18,32,128]{2,1,0:T(8,128)(2,1)S(1)}, bf16[18,32,128]{2,1,0:T(8,128)(2,1)S(1)}, u32[]{:S(2)}, u32[]{:S(2)}) collective-permute-start(bf16[18,32,128]{2,1,0:T(8,128)(2,1)S(1)} %get-tuple-element.17), channel_id=1, source_target_pairs={{0,8},{8,16},{16,24},{1,9},{9,17},{17,25},{2,10},{10,18},{18,26},{... | collective-permute-start | bytes 442376 | tf_op jit(solution)/shard_map/ppermute | solution.py:230
  90.3 0.0 collective-permute-done.1.down_ref
  90.3 1.0 collective-permute-done.up_ref
  91.2 0.3 pack.1
  91.5 4.9 %collective-permute-start.2 = (bf16[608,128]{1,0:T(8,128)(2,1)S(1)}, bf16[608,128]{1,0:T(8,128)(2,1)S(1)}, u32[]{:S(2)}, u32[]{:S(2)}) collective-permute-start(bf16[608,128]{1,0:T(8,128)(2,1)S(1)} %get-tuple-element.12), channel_id=1, source_target_pairs={{0,1},{1,2},{2,3},{3,4},{4,5},{5,6},{6,7},{8,9},{9,10},{10,11},{11... | collective-permute-start | bytes 466952 | tf_op jit(solution)/shard_map/ppermute | solution.py:230
  96.5 1.3 collective-permute-start.3
  97.8 2.1 %collective-permute-done.2.left_ref = bf16[608,128]{1,0:T(8,128)(2,1)S(1)} collective-permute-done((bf16[608,128]{1,0:T(8,128)(2,1)S(1)}, bf16[608,128]{1,0:T(8,128)(2,1)S(1)}, u32[]{:S(2)}, u32[]{:S(2)}) %collective-permute-start.2) | collective-permute-done | bytes 155680 | tf_op jit(solution)/shard_map/ppermute | solution.py:230
  99.9 6.2 %collective-permute-done.3.right_ref = bf16[608,128]{1,0:T(8,128)(2,1)S(1)} collective-permute-done((bf16[608,128]{1,0:T(8,128)(2,1)S(1)}, bf16[608,128]{1,0:T(8,128)(2,1)S(1)}, u32[]{:S(2)}, u32[]{:S(2)}) %collective-permute-start.3) | collective-permute-done | bytes 155680 | tf_op jit(solution)/shard_map/ppermute | solution.py:231
  106.1 0.0 copy-done.4
  106.1 14.9 %steps.1 = (f32[3,32,32,128]{3,2,1,0:T(8,128)}, f32[32,32,128]{2,1,0:T(8,128)S(1)}) custom-call(f32[3]{0:T(128)S(1)} %copy-done.4, bf16[3,32,32,128]{3,2,1,0:T(8,128)(2,1)S(1)} %copy-done, bf16[16,3,4,32,128]{4,3,2,1,0:T(8,128)(2,1)S(1)} %convert_element_type.7.lev_ref, bf16[18,32,128]{2,1,0:T(8,128)(2,1)S(1)} %collective-permute-done.up_ref, ...), custom_call_target="tpu_custom_call" | custom-call | tf_op jit(solution)/shard_map/steps/pallas_call | solution.py:292
  121.0 38.0 %all_to_all.11 = f32[16,2,32,128]{3,2,1,0:T(8,128)S(1)} all-to-all(f32[16,2,32,128]{3,2,1,0:T(8,128)S(1)} %bitcast.76), channel_id=1, replica_groups=mesh['rep'=16,'gx'=4,'gy'=8] {'rep'}, dimensions={0} | all-to-all | bytes 1048576 | tf_op jit(solution)/shard_map/all_to_all | solution.py:307
  159.0 0.6 reduce_sum.9
  (12 shorter events, 0.1 us)
Async XLA Ops:
  0.6 47.3 %copy-start = (bf16[3,32,32,128]{3,2,1,0:T(8,128)(2,1)S(1)}, bf16[3,32,32,128]{3,2,1,0:T(8,128)(2,1)}, u32[]{:S(2)}) copy-start(bf16[3,32,32,128]{3,2,1,0:T(8,128)(2,1)} %f_ref.1) | copy-start | bytes 2359300
  0.6 1.0 copy-start.1
  1.7 0.9 copy-start.2
  2.6 0.7 copy-start.3
  3.3 44.0 %copy-start.5 = (s32[3]{0:T(128)S(1)}, s32[3]{0:T(128)}, u32[]{:S(2)}) copy-start(s32[3]{0:T(128)} %levels_ref) | copy-start | bytes 40
  85.8 20.3 %copy-start.4 = (f32[3]{0:T(128)S(1)}, f32[3]{0:T(128)}, u32[]{:S(2)}) copy-start(f32[3]{0:T(128)} %coef_ref.1) | copy-start | bytes 40
  85.9 4.3 %collective-permute-start.1 = (bf16[18,32,128]{2,1,0:T(8,128)(2,1)S(1)}, bf16[18,32,128]{2,1,0:T(8,128)(2,1)S(1)}, u32[]{:S(2)}, u32[]{:S(2)}) collective-permute-start(bf16[18,32,128]{2,1,0:T(8,128)(2,1)S(1)} %get-tuple-element.16), channel_id=1, source_target_pairs={{8,0},{16,8},{24,16},{9,1},{17,9},{25,17},{10,2},{18,10},{26,18},{... | collective-permute-start | bytes 442376 | tf_op jit(solution)/shard_map/ppermute | solution.py:231
  87.2 4.0 %collective-permute-start = (bf16[18,32,128]{2,1,0:T(8,128)(2,1)S(1)}, bf16[18,32,128]{2,1,0:T(8,128)(2,1)S(1)}, u32[]{:S(2)}, u32[]{:S(2)}) collective-permute-start(bf16[18,32,128]{2,1,0:T(8,128)(2,1)S(1)} %get-tuple-element.17), channel_id=1, source_target_pairs={{0,8},{8,16},{16,24},{1,9},{9,17},{17,25},{2,10},{10,18},{18,26},{... | collective-permute-start | bytes 442376 | tf_op jit(solution)/shard_map/ppermute | solution.py:230
  91.5 8.4 %collective-permute-start.2 = (bf16[608,128]{1,0:T(8,128)(2,1)S(1)}, bf16[608,128]{1,0:T(8,128)(2,1)S(1)}, u32[]{:S(2)}, u32[]{:S(2)}) collective-permute-start(bf16[608,128]{1,0:T(8,128)(2,1)S(1)} %get-tuple-element.12), channel_id=1, source_target_pairs={{0,1},{1,2},{2,3},{3,4},{4,5},{5,6},{6,7},{8,9},{9,10},{10,11},{11... | collective-permute-start | bytes 466952 | tf_op jit(solution)/shard_map/ppermute | solution.py:230
  96.5 9.6 %collective-permute-start.3 = (bf16[608,128]{1,0:T(8,128)(2,1)S(1)}, bf16[608,128]{1,0:T(8,128)(2,1)S(1)}, u32[]{:S(2)}, u32[]{:S(2)}) collective-permute-start(bf16[608,128]{1,0:T(8,128)(2,1)S(1)} %get-tuple-element.13), channel_id=1, source_target_pairs={{1,0},{2,1},{3,2},{4,3},{5,4},{6,5},{7,6},{9,8},{10,9},{11,10},{12... | collective-permute-start | bytes 466952 | tf_op jit(solution)/shard_map/ppermute | solution.py:231

commit v3 on v2

--- a/solution.py
+++ b/solution.py
@@ -97,6 +97,17 @@
         out[k] = slices_ref[levels_ref[k]]
 
 
+def sweep(body, start, count, by=8):
+    def several(g, carry):
+        for i in range(by):
+            body(start + g * by + i, carry)
+        return carry
+
+    lax.fori_loop(0, count // by, several, 0)
+    for i in range(count // by * by, count):
+        body(start + i, 0)
+
+
 def steps_kernel(
     reps, rows, cols,
     coef_ref, f_ref, lev_ref, up_ref, down_ref, left_ref, right_ref,
@@ -169,7 +180,7 @@
                 put_tracer(at, lev_ref[g, k, own + i].astype(F32))
             return carry
 
-        lax.fori_loop(0, lev_ref.shape[0], level_rows, 0)
+        lax.fori_loop(0, lev_ref.shape[0], level_rows, 0, unroll=4)
         fill(put_speed, (0, k))
         fill(put_tracer, (1, k))
 
@@ -206,7 +217,7 @@
             return carry
 
         if k < STEPS - 1:
-            lax.fori_loop(k + 1, total - k, row, 0)
+            sweep(row, k + 1, total - 2 * k - 1)
 
     stretch = rows // sems.shape[0]
 
@@ -215,7 +226,7 @@
         return pltpu.make_async_copy(adj_ref.at[:, at], adj_hbm.at[:, at], sems.at[g])
 
     def some_rows(g, carry):
-        lax.fori_loop(REACH + 1 + g * stretch, REACH + 1 + (g + 1) * stretch, row, 0)
+        sweep(row, REACH + 1 + g * stretch, stretch)
         out_copy(g).start()
         return carry
 
@@ -248,7 +259,7 @@
         ],
         compiler_params=pltpu.CompilerParams(vmem_limit_bytes=8 * 2**20),
         name="own",
-    )(velocity, tracers, land_mask)
+    )(*(pltpu.with_memory_space_constraint(x, pltpu.HBM) for x in (velocity, tracers, land_mask)))
     slices = lax.all_to_all(mine, "rep", 0, 0, tiled=True)
     slices, forcing, step_levels = lax.optimization_barrier((slices, forcing, step_levels))
     picked = pl.pallas_call(

time: 160 us -> 150 us (0.938)
  Pallas kernels: 16.2 us -> 8.68 us
  local copies, waits for them, and re-layouts: 2.81 us -> 0.13 us
    pallas_call x1, Pallas kernels: 14.9 us -> 6.46 us  [local(): pl.pallas_call(functools.partial(steps_kernel, reps, rows, cols), out_sha...]
    unnamed x21 -> x15, local copies, waits for them, and re-layouts: 2.79 us -> 0.11 us
where the time goes in v3:
time: 150 us; the launch traced here: 149 us
  blocking collectives  119 us (79%)
  starting transfers between devices  10.6 us (7%)
  waiting for transfers between devices  9.31 us (6%)
  Pallas kernels  8.68 us (6%)
    all_to_all x1, blocking collectives, local(): slices = lax.all_to_all(mine, 'rep', 0, 0, tiled=True)  43.5 us
    all_to_all x1, blocking collectives, local(): lax.all_to_all(weighted.reshape(groups, own, cols, lanes), 'rep', 0, 0, t...  38 us
    all_gather x1, blocking collectives, local(): lev = lax.all_gather(picked.astype(jnp.float16), 'rep', axis=0, tiled=False)  37.5 us
    ppermute x2, starting transfers between devices, shift(): return lax.ppermute(x, axis, [(i, i + 1) for i in range(n - 1)])  7.98 us
    pallas_call x1, Pallas kernels, local(): pl.pallas_call(functools.partial(steps_kernel, reps, rows, cols), out_sha...  6.46 us
    ppermute x2, waiting for transfers between devices, shift(): return lax.ppermute(x, axis, [(i + 1, i) for i in range(n - 1)])  6.19 us
    ppermute x2, waiting for transfers between devices, shift(): return lax.ppermute(x, axis, [(i, i + 1) for i in range(n - 1)])  3.12 us
  transfers between devices with their start and end apart: 4, of which 3 were waited for; matrix products, arithmetic and copies ran while one was open for 0% of the time, Pallas kernels for 0%

profile of v3, /device:TPU:32, one launch (start us, length us, event | category | flops | bytes accessed | tf_op | source)
XLA Modules:
  0.0 149.5 jit_solution(10605212214267389283)
XLA Ops:
  0.6 0.0 copy-start.2
  0.6 0.0 copy-start
  0.7 1.4 own.1
  2.1 43.5 %all_to_all.10.slices_ref = bf16[16,4,32,128]{3,2,1,0:T(8,128)(2,1)S(1)} all-to-all(bf16[16,4,32,128]{3,2,1,0:T(8,128)(2,1)S(1)} %own.1), channel_id=1, replica_groups=mesh['rep'=16,'gx'=4,'gy'=8] {'rep'}, dimensions={0} | all-to-all | bytes 1048576 | tf_op jit(solution)/shard_map/all_to_all | solution.py:263
  45.6 0.0 copy-done.2
  45.6 0.6 pick.1
  46.2 0.0 copy-done
  46.2 37.5 %all-gather.2 = f16[48,4,32,128]{3,2,1,0:T(8,128)(2,1)S(1)} all-gather(f16[3,4,32,128]{3,2,1,0:T(8,128)(2,1)S(1)} %convert_element_type.6), channel_id=2, replica_groups=mesh['rep'=16,'gx'=4,'gy'=8] {'rep'}, dimensions={0}, use_global_device_ids=true | all-gather | bytes 1671168 | tf_op jit(solution)/shard_map/all_gather | solution.py:272
  83.7 0.3 convert_element_type.7.lev_ref
  84.0 0.0 copy-start.1
  84.2 1.3 collective-permute-start.1
  85.5 3.0 %collective-permute-start = (bf16[18,32,128]{2,1,0:T(8,128)(2,1)S(1)}, bf16[18,32,128]{2,1,0:T(8,128)(2,1)S(1)}, u32[]{:S(2)}, u32[]{:S(2)}) collective-permute-start(bf16[18,32,128]{2,1,0:T(8,128)(2,1)S(1)} %get-tuple-element.17), channel_id=1, source_target_pairs={{0,8},{8,16},{16,24},{1,9},{9,17},{17,25},{2,10},{10,18},{18,26},{... | collective-permute-start | bytes 442376 | tf_op jit(solution)/shard_map/ppermute | solution.py:241
  88.5 0.0 collective-permute-done.1.down_ref
  88.5 1.0 collective-permute-done.up_ref
  89.5 0.3 pack.1
  89.8 4.9 %collective-permute-start.2 = (bf16[608,128]{1,0:T(8,128)(2,1)S(1)}, bf16[608,128]{1,0:T(8,128)(2,1)S(1)}, u32[]{:S(2)}, u32[]{:S(2)}) collective-permute-start(bf16[608,128]{1,0:T(8,128)(2,1)S(1)} %get-tuple-element.12), channel_id=1, source_target_pairs={{0,1},{1,2},{2,3},{3,4},{4,5},{5,6},{6,7},{8,9},{9,10},{10,11},{11... | collective-permute-start | bytes 466952 | tf_op jit(solution)/shard_map/ppermute | solution.py:241
  94.7 1.3 collective-permute-start.3
  96.0 2.1 %collective-permute-done.2.left_ref = bf16[608,128]{1,0:T(8,128)(2,1)S(1)} collective-permute-done((bf16[608,128]{1,0:T(8,128)(2,1)S(1)}, bf16[608,128]{1,0:T(8,128)(2,1)S(1)}, u32[]{:S(2)}, u32[]{:S(2)}) %collective-permute-start.2) | collective-permute-done | bytes 155680 | tf_op jit(solution)/shard_map/ppermute | solution.py:241
  98.2 6.2 %collective-permute-done.3.right_ref = bf16[608,128]{1,0:T(8,128)(2,1)S(1)} collective-permute-done((bf16[608,128]{1,0:T(8,128)(2,1)S(1)}, bf16[608,128]{1,0:T(8,128)(2,1)S(1)}, u32[]{:S(2)}, u32[]{:S(2)}) %collective-permute-start.3) | collective-permute-done | bytes 155680 | tf_op jit(solution)/shard_map/ppermute | solution.py:242
  104.4 0.0 copy-done.1
  104.4 6.5 %steps.1 = (f32[3,32,32,128]{3,2,1,0:T(8,128)}, f32[32,32,128]{2,1,0:T(8,128)S(1)}) custom-call(f32[3]{0:T(128)S(1)} %copy-done.1, bf16[3,32,32,128]{3,2,1,0:T(8,128)(2,1)S(1)} %copy-done, bf16[16,3,4,32,128]{4,3,2,1,0:T(8,128)(2,1)S(1)} %convert_element_type.7.lev_ref, bf16[18,32,128]{2,1,0:T(8,128)(2,1)S(1)} %collective-permute-done.up_ref, ...), custom_call_target="tpu_custom_call" | custom-call | tf_op jit(solution)/shard_map/steps/pallas_call | solution.py:303
  110.8 38.0 %all_to_all.11 = f32[16,2,32,128]{3,2,1,0:T(8,128)S(1)} all-to-all(f32[16,2,32,128]{3,2,1,0:T(8,128)S(1)} %bitcast.76), channel_id=1, replica_groups=mesh['rep'=16,'gx'=4,'gy'=8] {'rep'}, dimensions={0} | all-to-all | bytes 1048576 | tf_op jit(solution)/shard_map/all_to_all | solution.py:318
  148.8 0.6 reduce_sum.9
  (12 shorter events, 0.1 us)
Async XLA Ops:
  0.6 44.9 %copy-start.2 = (s32[3]{0:T(128)S(1)}, s32[3]{0:T(128)}, u32[]{:S(2)}) copy-start(s32[3]{0:T(128)} %levels_ref) | copy-start | bytes 40
  0.6 45.5 %copy-start = (bf16[3,32,32,128]{3,2,1,0:T(8,128)(2,1)S(1)}, bf16[3,32,32,128]{3,2,1,0:T(8,128)(2,1)}, u32[]{:S(2)}) copy-start(bf16[3,32,32,128]{3,2,1,0:T(8,128)(2,1)} %f_ref.1) | copy-start | bytes 2359300
  84.0 20.3 %copy-start.1 = (f32[3]{0:T(128)S(1)}, f32[3]{0:T(128)}, u32[]{:S(2)}) copy-start(f32[3]{0:T(128)} %coef_ref.1) | copy-start | bytes 40
  84.2 4.3 %collective-permute-start.1 = (bf16[18,32,128]{2,1,0:T(8,128)(2,1)S(1)}, bf16[18,32,128]{2,1,0:T(8,128)(2,1)S(1)}, u32[]{:S(2)}, u32[]{:S(2)}) collective-permute-start(bf16[18,32,128]{2,1,0:T(8,128)(2,1)S(1)} %get-tuple-element.16), channel_id=1, source_target_pairs={{8,0},{16,8},{24,16},{9,1},{17,9},{25,17},{10,2},{18,10},{26,18},{... | collective-permute-start | bytes 442376 | tf_op jit(solution)/shard_map/ppermute | solution.py:242
  85.5 4.0 %collective-permute-start = (bf16[18,32,128]{2,1,0:T(8,128)(2,1)S(1)}, bf16[18,32,128]{2,1,0:T(8,128)(2,1)S(1)}, u32[]{:S(2)}, u32[]{:S(2)}) collective-permute-start(bf16[18,32,128]{2,1,0:T(8,128)(2,1)S(1)} %get-tuple-element.17), channel_id=1, source_target_pairs={{0,8},{8,16},{16,24},{1,9},{9,17},{17,25},{2,10},{10,18},{18,26},{... | collective-permute-start | bytes 442376 | tf_op jit(solution)/shard_map/ppermute | solution.py:241
  89.8 8.4 %collective-permute-start.2 = (bf16[608,128]{1,0:T(8,128)(2,1)S(1)}, bf16[608,128]{1,0:T(8,128)(2,1)S(1)}, u32[]{:S(2)}, u32[]{:S(2)}) collective-permute-start(bf16[608,128]{1,0:T(8,128)(2,1)S(1)} %get-tuple-element.12), channel_id=1, source_target_pairs={{0,1},{1,2},{2,3},{3,4},{4,5},{5,6},{6,7},{8,9},{9,10},{10,11},{11... | collective-permute-start | bytes 466952 | tf_op jit(solution)/shard_map/ppermute | solution.py:241
  94.7 9.6 %collective-permute-start.3 = (bf16[608,128]{1,0:T(8,128)(2,1)S(1)}, bf16[608,128]{1,0:T(8,128)(2,1)S(1)}, u32[]{:S(2)}, u32[]{:S(2)}) collective-permute-start(bf16[608,128]{1,0:T(8,128)(2,1)S(1)} %get-tuple-element.13), channel_id=1, source_target_pairs={{1,0},{2,1},{3,2},{4,3},{5,4},{6,5},{7,6},{9,8},{10,9},{11,10},{12... | collective-permute-start | bytes 466952 | tf_op jit(solution)/shard_map/ppermute | solution.py:242

commit v4 on v3

--- a/solution.py
+++ b/solution.py
@@ -11,9 +11,12 @@
 BF16 = jnp.bfloat16
 STEPS = 3
 REACH = 3
-WIDE = 40
 SCALE = 2.0**15
 DT = 0.1
+HALF = 64
+LAND = 4.0
+TALL = 38
+DEEP = 6
 
 LEVEL_HALO = ((0, 0, 3), (1, 0, 2), (0, 1, 2), (1, 1, 1), (0, 2, 1))
 
@@ -97,6 +100,29 @@
         out[k] = slices_ref[levels_ref[k]]
 
 
+def combine(coef_ref, news):
+    total = None
+    for r, new in enumerate(news):
+        part = coef_ref[r] * new
+        total = part if total is None else total + part
+    return total
+
+
+def speed_terms(v):
+    v = v * (0.5 * DT / SCALE)
+    o = pltpu.roll(v, HALF, axis=1)
+    low = lax.broadcasted_iota(jnp.int32, v.shape, 1) < HALF
+    return jnp.where(low, v, o), jnp.where(low, o, v)
+
+
+def tracer_terms(t):
+    return jnp.where(t > 0.0, (1.0 - 4.0 * DT) - DT * t, LAND), DT * pltpu.roll(t, HALF, axis=1)
+
+
+def edge_columns(k):
+    return (5 - k, 6 - k, 5 - k, 5 - k)
+
+
 def sweep(body, start, count, by=8):
     def several(g, carry):
         for i in range(by):
@@ -108,87 +134,72 @@
         body(start + i, 0)
 
 
-def steps_kernel(
+def inner_kernel(
     reps, rows, cols,
-    coef_ref, f_ref, lev_ref, up_ref, down_ref, left_ref, right_ref,
-    adj_hbm, sum_ref,
-    state, vx, vy, keep, swap, spare, adj_ref, sems,
+    coef_ref, f_ref, lev_ref, up_ref, down_ref,
+    adj_hbm, sum_ref, edge_state, edge_terms, tiles,
+    state, vx, vy, keep, swap, adj_ref, sems,
 ):
     xi, _ = x_index(reps)
-    strips, corners = y_index(reps)
     total = rows + 2 * REACH
-    base = len(strips) * rows
-    half = 64
-    extra = spare.shape[0] // 2
-
-    def put_state(r):
-        def put(at, v):
-            state[0, r, at, :] = v
-
-        return put
-
-    def put_speed(at, v):
-        v = v * (0.5 * DT / SCALE)
-        o = pltpu.roll(v, half, axis=1)
-        is_low = lax.broadcasted_iota(jnp.int32, v.shape, 1) < half
-        vx[at, :] = jnp.where(is_low, v, o)
-        vy[at, :] = jnp.where(is_low, o, v)
-
-    def put_tracer(at, t):
-        keep[at, :] = jnp.where(t > 0.0, (1.0 - 4.0 * DT) - DT * t, 4.0)
-        swap[at, :] = DT * pltpu.roll(t, half, axis=1)
-
-    def fill(put, key):
+    own = lev_ref.shape[2] // 2
+
+    def slot(x):
+        return pl.ds(pl.multiple_of((x + 1) * cols, 8), cols)
+
+    def put_speed(x, v):
+        vx[slot(x), :], vy[slot(x), :] = speed_terms(v)
+
+    def put_tracer(x, t):
+        keep[slot(x), :], swap[slot(x), :] = tracer_terms(t)
+
+    def put_rows(put, key):
         if key in xi:
             first, width = xi[key]
             for e in range(1, width + 1):
-                put(pl.ds((REACH - e + 1) * WIDE, cols), up_ref[first + width - e].astype(F32))
-                put(pl.ds((REACH + rows + e) * WIDE, cols), down_ref[first + e - 1].astype(F32))
-        for side, source in ((0, left_ref), (1, right_ref)):
-            for n, (k, d) in enumerate(strips):
-                if k == key:
-                    c = -d if side == 0 else cols + d - 1
-                    at = pl.ds((REACH + 1) * WIDE + c, rows, stride=WIDE)
-                    put(at, source[pl.ds(n * rows, rows), :].astype(F32))
-            for n, (k, d, e, edge) in enumerate(corners):
-                if k == key:
-                    c = -d if side == 0 else cols + d - 1
-                    x = REACH - e if edge == 0 else REACH + rows + e - 1
-                    put(pl.ds((x + 1) * WIDE + c, 1), spare[pl.ds(side * extra + n, 1), :])
-
-    spare[pl.ds(0, extra), :] = left_ref[pl.ds(base, extra), :].astype(F32)
-    spare[pl.ds(extra, extra), :] = right_ref[pl.ds(base, extra), :].astype(F32)
+                put(REACH - e, up_ref[first + width - e].astype(F32))
+                put(REACH + rows + e - 1, down_ref[first + e - 1].astype(F32))
 
     def forcing_row(x, carry):
-        at = pl.ds(pl.multiple_of((x + REACH + 1) * WIDE, 8), cols)
         for r in range(reps):
-            state[0, r, at, :] = f_ref[r, x].astype(F32)
+            state[0, r, slot(x + REACH), :] = f_ref[r, x].astype(F32)
         return carry
 
     lax.fori_loop(0, rows, forcing_row, 0, unroll=4)
     for r in range(reps):
-        fill(put_state(r), ("f", r))
+
+        def put_state(x, v, r=r):
+            state[0, r, slot(x), :] = v
+
+        put_rows(put_state, ("f", r))
+        for side in (0, 1):
+            for depth in range(edge_state.shape[2]):
+                y = depth if side == 0 else cols - 1 - depth
+                edge_state[side, r, depth] = state[0, r, pl.ds(cols + y, TALL, stride=cols), :]
 
     for k in range(STEPS):
         now, later = k % 2, (k + 1) % 2
 
         def level_rows(g, carry, k=k):
-            own = lev_ref.shape[2] // 2
             for i in range(own):
-                at = pl.ds(pl.multiple_of((g * own + i + REACH + 1) * WIDE, 8), cols)
-                put_speed(at, lev_ref[g, k, i].astype(F32))
-                put_tracer(at, lev_ref[g, k, own + i].astype(F32))
+                put_speed(g * own + i + REACH, lev_ref[g, k, i].astype(F32))
+                put_tracer(g * own + i + REACH, lev_ref[g, k, own + i].astype(F32))
             return carry
 
         lax.fori_loop(0, lev_ref.shape[0], level_rows, 0, unroll=4)
-        fill(put_speed, (0, k))
-        fill(put_tracer, (1, k))
+        put_rows(put_speed, (0, k))
+        put_rows(put_tracer, (1, k))
+        for side in (0, 1):
+            for n, (source, count) in enumerate(zip((vx, vy, keep, swap), edge_columns(k))):
+                for depth in range(count):
+                    y = depth if side == 0 else cols - 1 - depth
+                    edge_terms[side, k, n, depth] = source[pl.ds(cols + y, TALL, stride=cols), :]
 
         def row(x, carry, k=k, now=now, later=later):
-            start = pl.multiple_of(x * WIDE, 8)
-            for j in range(0, cols if k == STEPS - 1 else WIDE, 8):
+            start = pl.multiple_of((x + 1) * cols, 8)
+            for j in range(0, cols, 8):
                 at = pl.ds(start + j, 8)
-                above, below = pl.ds(start + j - WIDE, 8), pl.ds(start + j + WIDE, 8)
+                above, below = pl.ds(start + j - cols, 8), pl.ds(start + j + cols, 8)
                 before, after = pl.ds(start + j - 1, 8), pl.ds(start + j + 1, 8)
                 a = DT + vx[above, :]
                 b = DT - vx[below, :]
@@ -197,42 +208,123 @@
                 centre = keep[at, :]
                 other = swap[at, :]
                 ocean = centre < 1.0
-                weighted = None
+                news = []
                 for r in range(reps):
                     s = state[now, r, at, :]
                     new = (
                         (a * state[now, r, above, :] + b * state[now, r, below, :])
                         + (c * state[now, r, before, :] + d * state[now, r, after, :])
-                        + (centre * s + other * pltpu.roll(s, half, axis=1))
+                        + (centre * s + other * pltpu.roll(s, HALF, axis=1))
                     )
                     new = jnp.where(ocean, new, 0.0)
                     if k < STEPS - 1:
                         state[later, r, at, :] = new
                     else:
-                        adj_ref[r, x - REACH - 1, pl.ds(j, 8)] = new
-                        part = coef_ref[r] * new
-                        weighted = part if weighted is None else weighted + part
-                if k == STEPS - 1:
-                    sum_ref[x - REACH - 1, pl.ds(j, 8)] = weighted
+                        adj_ref[r, pl.ds(pl.multiple_of((x - REACH) * cols, 8) + j, 8), :] = new
+                        if j in (0, cols - 8):
+                            tiles[min(j, 1), r, pl.ds(pl.multiple_of((x - REACH) * 8, 8), 8), :] = new
+                        news.append(new)
+                if news:
+                    sum_ref[pl.ds(pl.multiple_of((x - REACH) * cols, 8) + j, 8), :] = combine(coef_ref, news)
             return carry
 
         if k < STEPS - 1:
-            sweep(row, k + 1, total - 2 * k - 1)
+            sweep(row, k + 1, total - 2 * k - 2)
 
     stretch = rows // sems.shape[0]
 
     def out_copy(g):
-        at = pl.ds(g * stretch, stretch)
+        at = pl.ds(g * stretch * cols, stretch * cols)
         return pltpu.make_async_copy(adj_ref.at[:, at], adj_hbm.at[:, at], sems.at[g])
 
     def some_rows(g, carry):
-        sweep(row, REACH + 1 + g * stretch, stretch)
+        sweep(row, REACH + g * stretch, stretch)
         out_copy(g).start()
         return carry
 
     lax.fori_loop(0, sems.shape[0], some_rows, 0)
     for g in range(sems.shape[0]):
         out_copy(g).wait()
+
+
+def edge_kernel(
+    reps, rows, cols,
+    coef_ref, edge_state, edge_terms, left_ref, right_ref, tiles_in, adj_in, sum_in,
+    tiles, adj_hbm, sum_ref,
+    halo_state, halo_terms, state, spare, sems,
+):
+    del tiles_in, adj_in, sum_in
+    strips, corners = y_index(reps)
+    base = len(strips) * rows
+    extra = spare.shape[0]
+
+    def out_copy(side):
+        target = adj_hbm.at[:, :, pl.ds(side * (cols - 8), 8)]
+        return pltpu.make_async_copy(tiles.at[side].reshape(reps, rows, 8, 128), target, sems.at[side])
+
+    for side, source in ((0, left_ref), (1, right_ref)):
+        spare[...] = source[pl.ds(base, extra), :].astype(F32)
+
+        def put(key, q, at, v, side=side):
+            if key[0] == "f":
+                halo_state[side, key[1], q, at, :] = v
+            elif key[0] == 0:
+                halo_terms[side, key[1], 0, q, at, :], halo_terms[side, key[1], 1, q, at, :] = speed_terms(v)
+            else:
+                halo_terms[side, key[1], 2, q, at, :], halo_terms[side, key[1], 3, q, at, :] = tracer_terms(v)
+
+        for n, (key, d) in enumerate(strips):
+            put(key, REACH - d, pl.ds(8 + REACH, rows), source[pl.ds(n * rows, rows), :].astype(F32))
+        for n, (key, d, e, edge) in enumerate(corners):
+            x = REACH - e if edge == 0 else REACH + rows + e - 1
+            put(key, REACH - d, pl.ds(8 + x, 1), spare[pl.ds(n, 1), :])
+
+        sign = 1.0 if side == 0 else -1.0
+
+        def term(k, n, q, start, size, side=side):
+            if q < REACH:
+                return halo_terms[side, k, n, q, pl.ds(8 + start, size), :]
+            return edge_terms[side, k, n, q - REACH, pl.ds(start, size), :]
+
+        def cell(k, r, q, start, size, side=side):
+            if k > 0:
+                return state[(k - 1) % 2, r, q, pl.ds(8 + start, size), :]
+            if q < REACH:
+                return halo_state[side, r, q, pl.ds(8 + start, size), :]
+            return edge_state[side, r, q - REACH, pl.ds(start, size), :]
+
+        for k in range(STEPS):
+            for q in range(k + 1, 8 - k):
+                for start in range(k + 1, k + 1 + rows + 2 * (REACH - k - 1), 8):
+                    size = min(8, k + 1 + rows + 2 * (REACH - k - 1) - start)
+                    a = DT + term(k, 0, q, start - 1, size)
+                    b = DT - term(k, 0, q, start + 1, size)
+                    c = DT + sign * term(k, 1, q - 1, start, size)
+                    d = DT - sign * term(k, 1, q + 1, start, size)
+                    centre = term(k, 2, q, start, size)
+                    other = term(k, 3, q, start, size)
+                    ocean = centre < 1.0
+                    news = []
+                    for r in range(reps):
+                        s = cell(k, r, q, start, size)
+                        new = (
+                            (a * cell(k, r, q, start - 1, size) + b * cell(k, r, q, start + 1, size))
+                            + (c * cell(k, r, q - 1, start, size) + d * cell(k, r, q + 1, start, size))
+                            + (centre * s + other * pltpu.roll(s, HALF, axis=1))
+                        )
+                        new = jnp.where(ocean, new, 0.0)
+                        if k < STEPS - 1:
+                            state[k % 2, r, q, pl.ds(8 + start, size), :] = new
+                        news.append(new)
+                    if k == STEPS - 1:
+                        y = q - REACH if side == 0 else cols - 1 - (q - REACH)
+                        sum_ref[pl.ds((start - REACH) * cols + y, size, stride=cols), :] = combine(coef_ref, news)
+                        y = q - REACH if side == 0 else 7 - (q - REACH)
+                        for r in range(reps):
+                            tiles[side, r, pl.ds((start - REACH) * 8 + y, size, stride=8), :] = news[r]
+        out_copy(side).start()
+    for side in (0, 1):
+        out_copy(side).wait()
 
 
 def shift(x, axis, by):
@@ -299,21 +391,45 @@
     left = shift(to_right, "gy", 1)
 
     vm = pl.BlockSpec(memory_space=pltpu.VMEM)
-    size = (rows + 2 * REACH + 2) * WIDE
-    adjoints, weighted = pl.pallas_call(
-        functools.partial(steps_kernel, reps, rows, cols),
+    sm = pl.BlockSpec(memory_space=pltpu.SMEM)
+    size = (rows + 2 * REACH + 2) * cols
+    total = jax.ShapeDtypeStruct((rows * cols, lanes), F32)
+    tiled = jax.ShapeDtypeStruct((2, reps, rows * 8, lanes), F32)
+    adjoints, weighted, edge_state, edge_terms, tiles = pl.pallas_call(
+        functools.partial(inner_kernel, reps, rows, cols),
         out_shape=(
-            jax.ShapeDtypeStruct((reps, rows, cols, lanes), F32),
-            jax.ShapeDtypeStruct((rows, cols, lanes), F32),
+            jax.ShapeDtypeStruct((reps, rows * cols, lanes), F32),
+            total,
+            jax.ShapeDtypeStruct((2, reps, DEEP, TALL, lanes), F32),
+            jax.ShapeDtypeStruct((2, STEPS, 4, DEEP, TALL, lanes), F32),
+            tiled,
         ),
-        in_specs=[pl.BlockSpec(memory_space=pltpu.SMEM)] + [vm] * 6,
-        out_specs=(hbm, vm),
+        in_specs=[sm] + [vm] * 4,
+        out_specs=(hbm,) + (vm,) * 4,
         scratch_shapes=[pltpu.VMEM((2, reps, size, lanes), F32)]
         + [pltpu.VMEM((size, lanes), F32)] * 4
-        + [pltpu.VMEM((2 * extra, lanes), F32), pltpu.VMEM((reps, rows, cols, lanes), F32), pltpu.SemaphoreType.DMA((4,))],
+        + [pltpu.VMEM((reps, rows * cols, lanes), F32), pltpu.SemaphoreType.DMA((4,))],
         compiler_params=pltpu.CompilerParams(vmem_limit_bytes=24 * 2**20),
-        name="steps",
-    )(coefficients, forcing, lev, up, down, left, right)
+        name="inner",
+    )(coefficients, forcing, lev, up, down)
+    adjoints = adjoints.reshape(reps, rows, cols, lanes)
+    long = 8 + TALL + 2
+    _, adjoints, weighted = pl.pallas_call(
+        functools.partial(edge_kernel, reps, rows, cols),
+        out_shape=(tiled, jax.ShapeDtypeStruct(adjoints.shape, F32), total),
+        in_specs=[sm] + [vm] * 5 + [hbm, vm],
+        out_specs=(vm, hbm, vm),
+        scratch_shapes=[
+            pltpu.VMEM((2, reps, REACH, long, lanes), F32),
+            pltpu.VMEM((2, STEPS, 4, REACH, long, lanes), F32),
+            pltpu.VMEM((2, reps, REACH + DEEP, long, lanes), F32),
+            pltpu.VMEM((extra, lanes), F32),
+            pltpu.SemaphoreType.DMA((2,)),
+        ],
+        input_output_aliases={5: 0, 6: 1, 7: 2},
+        compiler_params=pltpu.CompilerParams(vmem_limit_bytes=12 * 2**20),
+        name="edge",
+    )(coefficients, edge_state, edge_terms, left, right, tiles, adjoints, weighted)
 
     parts = lax.all_to_all(weighted.reshape(groups, own, cols, lanes), "rep", 0, 0, tiled=True)
     return jnp.sum(parts, axis=0), adjoints

time: 150 us -> 147 us (0.980)
  the two profiles are of different devices: /device:TPU:32 before, /device:TPU:25 now
where the time goes in v4:
time: 147 us
  blocking collectives  108 us (73%)
  starting transfers between devices  22.9 us (16%)
  Pallas kernels  12.2 us (8%)
  waiting for transfers between devices  2.08 us (1%)
    all_to_all x1, blocking collectives, local(): slices = lax.all_to_all(mine, 'rep', 0, 0, tiled=True)  37.7 us
    all_gather x1, blocking collectives, local(): lev = lax.all_gather(picked.astype(jnp.float16), 'rep', axis=0, tiled=False)  37.1 us
    all_to_all x1, blocking collectives, local(): lax.all_to_all(weighted.reshape(groups, own, cols, lanes), 'rep', 0, 0, t...  32.8 us
    ppermute x2, starting transfers between devices, shift(): return lax.ppermute(x, axis, [(i + 1, i) for i in range(n - 1)])  15.6 us
    ppermute x2, starting transfers between devices, shift(): return lax.ppermute(x, axis, [(i, i + 1) for i in range(n - 1)])  7.38 us
    pallas_call x1, Pallas kernels, local(): pl.pallas_call(functools.partial(inner_kernel, reps, rows, cols), out_sha...  7.32 us
  transfers between devices with their start and end apart: 4, of which 2 were waited for; matrix products, arithmetic and copies ran while one was open for 0% of the time, Pallas kernels for 5%

profile of v4, /device:TPU:25, one launch (start us, length us, event | category | flops | bytes accessed | tf_op | source)
XLA Modules:
  0.0 146.8 jit_solution(15749270517513808914)
XLA Ops:
  0.6 0.0 copy-start.2
  0.6 0.0 copy-start
  0.7 1.4 own.1
  2.1 37.7 %all_to_all.10.slices_ref = bf16[16,4,32,128]{3,2,1,0:T(8,128)(2,1)S(1)} all-to-all(bf16[16,4,32,128]{3,2,1,0:T(8,128)(2,1)S(1)} %own.1), channel_id=1, replica_groups=mesh['rep'=16,'gx'=4,'gy'=8] {'rep'}, dimensions={0} | all-to-all | bytes 1048576 | tf_op jit(solution)/shard_map/all_to_all | solution.py:355
  39.8 0.0 copy-done.2
  39.8 0.6 pick.1
  40.4 0.0 copy-done
  40.4 37.1 %all-gather.2 = f16[48,4,32,128]{3,2,1,0:T(8,128)(2,1)S(1)} all-gather(f16[3,4,32,128]{3,2,1,0:T(8,128)(2,1)S(1)} %convert_element_type.6), channel_id=2, replica_groups=mesh['rep'=16,'gx'=4,'gy'=8] {'rep'}, dimensions={0}, use_global_device_ids=true | all-gather | bytes 1671168 | tf_op jit(solution)/shard_map/all_gather | solution.py:364
  77.5 0.3 convert_element_type.7.lev_ref
  77.9 0.0 copy-start.1
  78.0 12.2 %collective-permute-start.1 = (bf16[18,32,128]{2,1,0:T(8,128)(2,1)S(1)}, bf16[18,32,128]{2,1,0:T(8,128)(2,1)S(1)}, u32[]{:S(2)}, u32[]{:S(2)}) collective-permute-start(bf16[18,32,128]{2,1,0:T(8,128)(2,1)S(1)} %get-tuple-element.26), channel_id=1, source_target_pairs={{8,0},{16,8},{24,16},{9,1},{17,9},{25,17},{10,2},{18,10},{26,18},{... | collective-permute-start | bytes 442376 | tf_op jit(solution)/shard_map/ppermute | solution.py:334
  90.3 3.0 %collective-permute-start = (bf16[18,32,128]{2,1,0:T(8,128)(2,1)S(1)}, bf16[18,32,128]{2,1,0:T(8,128)(2,1)S(1)}, u32[]{:S(2)}, u32[]{:S(2)}) collective-permute-start(bf16[18,32,128]{2,1,0:T(8,128)(2,1)S(1)} %get-tuple-element.27), channel_id=1, source_target_pairs={{0,8},{8,16},{16,24},{1,9},{9,17},{17,25},{2,10},{10,18},{18,26},{... | collective-permute-start | bytes 442376 | tf_op jit(solution)/shard_map/ppermute | solution.py:333
  93.3 0.9 collective-permute-done.1.down_ref
  94.2 1.2 collective-permute-done.up_ref
  95.4 0.3 pack.1
  95.6 4.4 %collective-permute-start.2 = (bf16[608,128]{1,0:T(8,128)(2,1)S(1)}, bf16[608,128]{1,0:T(8,128)(2,1)S(1)}, u32[]{:S(2)}, u32[]{:S(2)}) collective-permute-start(bf16[608,128]{1,0:T(8,128)(2,1)S(1)} %get-tuple-element.19), channel_id=1, source_target_pairs={{0,1},{1,2},{2,3},{3,4},{4,5},{5,6},{6,7},{8,9},{9,10},{10,11},{11... | collective-permute-start | bytes 466952 | tf_op jit(solution)/shard_map/ppermute | solution.py:333
  100.0 3.3 %collective-permute-start.3 = (bf16[608,128]{1,0:T(8,128)(2,1)S(1)}, bf16[608,128]{1,0:T(8,128)(2,1)S(1)}, u32[]{:S(2)}, u32[]{:S(2)}) collective-permute-start(bf16[608,128]{1,0:T(8,128)(2,1)S(1)} %get-tuple-element.20), channel_id=1, source_target_pairs={{1,0},{2,1},{3,2},{4,3},{5,4},{6,5},{7,6},{9,8},{10,9},{11,10},{12... | collective-permute-start | bytes 466952 | tf_op jit(solution)/shard_map/ppermute | solution.py:334
  103.3 0.0 copy-done.1
  103.4 7.3 %inner.1 = (f32[3,1024,128]{2,1,0:T(8,128)}, f32[1024,128]{1,0:T(8,128)S(1)}, f32[2,3,6,38,128]{4,3,2,1,0:T(8,128)S(1)}, f32[2,3,4,6,38,128]{5,4,3,2,1,0:T(8,128)S(1)}, f32[2,3,256,128]{3,2,1,0:T(8,128)S(1)}) custom-call(f32[3]{0:T(128)S(1)} %copy-done.1, bf16[3,32,32,128]{3,2,1,0:T(8,128)(2,1)S(1)} %copy-done, ...), custom_call_target="tpu_custom_call" | custom-call | tf_op jit(solution)/shard_map/inner/pallas_call | solution.py:398
  110.7 0.0 collective-permute-done.2.left_ref
  110.7 0.0 collective-permute-done.3.right_ref
  110.7 2.6 %edge.1 = (f32[2,3,256,128]{3,2,1,0:T(8,128)S(1)}, f32[3,32,32,128]{3,2,1,0:T(8,128)}, f32[1024,128]{1,0:T(8,128)S(1)}) custom-call(f32[3]{0:T(128)S(1)} %copy-done.1, f32[2,3,6,38,128]{4,3,2,1,0:T(8,128)S(1)} %get-tuple-element.17.edge_state, ...), custom_call_target="tpu_custom_call", output_to_operand_aliasing={{0}: (5, {}), {1}: (6, {}), {2}: (7, {})} | custom-call | tf_op jit(solution)/shard_map/edge/pallas_call | solution.py:417
  113.4 32.8 %all_to_all.11 = f32[16,2,32,128]{3,2,1,0:T(8,128)S(1)} all-to-all(f32[16,2,32,128]{3,2,1,0:T(8,128)S(1)} %bitcast.77), channel_id=1, replica_groups=mesh['rep'=16,'gx'=4,'gy'=8] {'rep'}, dimensions={0} | all-to-all | bytes 1048576 | tf_op jit(solution)/shard_map/all_to_all | solution.py:434
  146.2 0.6 reduce_sum.9
  (12 shorter events, 0.1 us)
Async XLA Ops:
  0.6 39.1 %copy-start.2 = (s32[3]{0:T(128)S(1)}, s32[3]{0:T(128)}, u32[]{:S(2)}) copy-start(s32[3]{0:T(128)} %levels_ref) | copy-start | bytes 40
  0.6 39.7 %copy-start = (bf16[3,32,32,128]{3,2,1,0:T(8,128)(2,1)S(1)}, bf16[3,32,32,128]{3,2,1,0:T(8,128)(2,1)}, u32[]{:S(2)}) copy-start(bf16[3,32,32,128]{3,2,1,0:T(8,128)(2,1)} %f_ref.1) | copy-start | bytes 2359300
  77.9 25.5 %copy-start.1 = (f32[3]{0:T(128)S(1)}, f32[3]{0:T(128)}, u32[]{:S(2)}) copy-start(f32[3]{0:T(128)} %coef_ref.3) | copy-start | bytes 40
  78.0 16.2 %collective-permute-start.1 = (bf16[18,32,128]{2,1,0:T(8,128)(2,1)S(1)}, bf16[18,32,128]{2,1,0:T(8,128)(2,1)S(1)}, u32[]{:S(2)}, u32[]{:S(2)}) collective-permute-start(bf16[18,32,128]{2,1,0:T(8,128)(2,1)S(1)} %get-tuple-element.26), channel_id=1, source_target_pairs={{8,0},{16,8},{24,16},{9,1},{17,9},{25,17},{10,2},{18,10},{26,18},{... | collective-permute-start | bytes 442376 | tf_op jit(solution)/shard_map/ppermute | solution.py:334
  90.3 5.1 %collective-permute-start = (bf16[18,32,128]{2,1,0:T(8,128)(2,1)S(1)}, bf16[18,32,128]{2,1,0:T(8,128)(2,1)S(1)}, u32[]{:S(2)}, u32[]{:S(2)}) collective-permute-start(bf16[18,32,128]{2,1,0:T(8,128)(2,1)S(1)} %get-tuple-element.27), channel_id=1, source_target_pairs={{0,8},{8,16},{16,24},{1,9},{9,17},{17,25},{2,10},{10,18},{18,26},{... | collective-permute-start | bytes 442376 | tf_op jit(solution)/shard_map/ppermute | solution.py:333
  95.6 15.0 %collective-permute-start.2 = (bf16[608,128]{1,0:T(8,128)(2,1)S(1)}, bf16[608,128]{1,0:T(8,128)(2,1)S(1)}, u32[]{:S(2)}, u32[]{:S(2)}) collective-permute-start(bf16[608,128]{1,0:T(8,128)(2,1)S(1)} %get-tuple-element.19), channel_id=1, source_target_pairs={{0,1},{1,2},{2,3},{3,4},{4,5},{5,6},{6,7},{8,9},{9,10},{10,11},{11... | collective-permute-start | bytes 466952 | tf_op jit(solution)/shard_map/ppermute | solution.py:333
  100.0 10.7 %collective-permute-start.3 = (bf16[608,128]{1,0:T(8,128)(2,1)S(1)}, bf16[608,128]{1,0:T(8,128)(2,1)S(1)}, u32[]{:S(2)}, u32[]{:S(2)}) collective-permute-start(bf16[608,128]{1,0:T(8,128)(2,1)S(1)} %get-tuple-element.20), channel_id=1, source_target_pairs={{1,0},{2,1},{3,2},{4,3},{5,4},{6,5},{7,6},{9,8},{10,9},{11,10},{12... | collective-permute-start | bytes 466952 | tf_op jit(solution)/shard_map/ppermute | solution.py:334

commit v5 on v4

--- a/solution.py
+++ b/solution.py
@@ -47,7 +47,12 @@
     return strips, corners
 
 
-def pack_kernel(reps, rows, cols, f_ref, lev_ref, up_ref, down_ref, left_ref, right_ref, tile, out):
+def swaps(x, axis, first):
+    ends = lax.axis_size(axis) - 1
+    return lax.ppermute(x, axis, [p for i in range(first, ends, 2) for p in ((i, i + 1), (i + 1, i))])
+
+
+def pack_kernel(reps, rows, cols, f_ref, lev_ref, up_ref, down_ref, even_ref, odd_ref, both, tile, out):
     xi, _ = x_index(reps)
     strips, corners = y_index(reps)
     keys = []
@@ -55,7 +60,8 @@
         if key not in keys:
             keys.append(key)
     base = len(strips) * rows
-    for side, target in ((0, left_ref), (1, right_ref)):
+    for side in (0, 1):
+        target = both.at[side]
         lo = 0 if side == 0 else cols - 8
         for key in keys:
             for x in range(rows):
@@ -75,6 +81,9 @@
             c = d - 1 if side == 0 else 8 - d
             out[pl.ds(n, 1), :] = row.astype(F32)[c : c + 1]
         target[pl.ds(base, out.shape[0]), :] = out[...].astype(target.dtype)
+    parity = lax.rem(lax.axis_index("gy"), 2)
+    even_ref[...] = both[1 - parity]
+    odd_ref[...] = both[parity]
 
 
 def own_kernel(groups, own, v_hbm, t_hbm, mask_hbm, out, v_ref, t_ref, mask_ref, sems):
@@ -249,9 +258,9 @@
 
 def edge_kernel(
     reps, rows, cols,
-    coef_ref, edge_state, edge_terms, left_ref, right_ref, tiles_in, adj_in, sum_in,
+    coef_ref, edge_state, edge_terms, odd_ref, even_ref, tiles_in, adj_in, sum_in,
     tiles, adj_hbm, sum_ref,
-    halo_state, halo_terms, state, spare, sems,
+    got, halo_state, halo_terms, state, spare, sems,
 ):
     del tiles_in, adj_in, sum_in
     strips, corners = y_index(reps)
@@ -262,7 +271,11 @@
         target = adj_hbm.at[:, :, pl.ds(side * (cols - 8), 8)]
         return pltpu.make_async_copy(tiles.at[side].reshape(reps, rows, 8, 128), target, sems.at[side])
 
-    for side, source in ((0, left_ref), (1, right_ref)):
+    parity = lax.rem(lax.axis_index("gy"), 2)
+    got[0] = even_ref[...]
+    got[1] = odd_ref[...]
+    for side in (0, 1):
+        source = got.at[1 - parity if side == 0 else parity]
         spare[...] = source[pl.ds(base, extra), :].astype(F32)
 
         def put(key, q, at, v, side=side):
@@ -380,15 +393,19 @@
     extra = -(-len(corners) // 16) * 16
     length = len(strips) * rows + extra
     payload = jax.ShapeDtypeStruct((length, lanes), BF16)
-    to_left, to_right = pl.pallas_call(
+    to_even, to_odd = pl.pallas_call(
         functools.partial(pack_kernel, reps, rows, cols),
         out_shape=(payload, payload),
-        scratch_shapes=[pltpu.VMEM((rows * 8, lanes), F32), pltpu.VMEM((extra, lanes), F32)],
+        scratch_shapes=[
+            pltpu.VMEM((2, length, lanes), BF16),
+            pltpu.VMEM((rows * 8, lanes), F32),
+            pltpu.VMEM((extra, lanes), F32),
+        ],
         compiler_params=pltpu.CompilerParams(vmem_limit_bytes=8 * 2**20),
         name="pack",
     )(forcing, lev, up, down)
-    right = shift(to_left, "gy", -1)
-    left = shift(to_right, "gy", 1)
+    odd = swaps(to_odd, "gy", 1)
+    even = swaps(to_even, "gy", 0)
 
     vm = pl.BlockSpec(memory_space=pltpu.VMEM)
     sm = pl.BlockSpec(memory_space=pltpu.SMEM)
@@ -420,6 +437,7 @@
         in_specs=[sm] + [vm] * 5 + [hbm, vm],
         out_specs=(vm, hbm, vm),
         scratch_shapes=[
+            pltpu.VMEM((2, length, lanes), BF16),
             pltpu.VMEM((2, reps, REACH, long, lanes), F32),
             pltpu.VMEM((2, STEPS, 4, REACH, long, lanes), F32),
             pltpu.VMEM((2, reps, REACH + DEEP, long, lanes), F32),
@@ -429,7 +447,7 @@
         input_output_aliases={5: 0, 6: 1, 7: 2},
         compiler_params=pltpu.CompilerParams(vmem_limit_bytes=12 * 2**20),
         name="edge",
-    )(coefficients, edge_state, edge_terms, left, right, tiles, adjoints, weighted)
+    )(coefficients, edge_state, edge_terms, odd, even, tiles, adjoints, weighted)
 
     parts = lax.all_to_all(weighted.reshape(groups, own, cols, lanes), "rep", 0, 0, tiled=True)
     return jnp.sum(parts, axis=0), adjoints

time: 147 us -> 148 us (level)
  the two profiles are of different devices: /device:TPU:25 before, /device:TPU:1 now
where the time goes in v5:
time: 148 us
  blocking collectives  108 us (73%)
  starting transfers between devices  23.1 us (16%)
  Pallas kernels  12.2 us (8%)
  waiting for transfers between devices  2.08 us (1%)
    all_to_all x1, blocking collectives, local(): slices = lax.all_to_all(mine, 'rep', 0, 0, tiled=True)  38.5 us
    all_gather x1, blocking collectives, local(): lev = lax.all_gather(picked.astype(jnp.float16), 'rep', axis=0, tiled=False)  37.1 us
    all_to_all x1, blocking collectives, local(): lax.all_to_all(weighted.reshape(groups, own, cols, lanes), 'rep', 0, 0, t...  32.8 us
    ppermute x1, starting transfers between devices, shift(): return lax.ppermute(x, axis, [(i + 1, i) for i in range(n - 1)])  12.2 us
    ppermute x2, starting transfers between devices, swaps(): lax.ppermute(x, axis, [p for i in range(first, ends, 2) for p in ((i, i +...  7.8 us
    pallas_call x1, Pallas kernels, local(): pl.pallas_call(functools.partial(inner_kernel, reps, rows, cols), out_sha...  7.32 us
    ppermute x1, starting transfers between devices, shift(): return lax.ppermute(x, axis, [(i, i + 1) for i in range(n - 1)])  3.02 us
  transfers between devices with their start and end apart: 4, of which 2 were waited for; matrix products, arithmetic and copies ran while one was open for 0% of the time, Pallas kernels for 5%

profile of v5, /device:TPU:1, one launch (start us, length us, event | category | flops | bytes accessed | tf_op | source)
XLA Modules:
  0.0 147.8 jit_solution(9544104539050716314)
XLA Ops:
  0.6 0.0 copy-start.2
  0.6 0.0 copy-start
  0.7 1.4 own.1
  2.1 38.5 %all_to_all.10.slices_ref = bf16[16,4,32,128]{3,2,1,0:T(8,128)(2,1)S(1)} all-to-all(bf16[16,4,32,128]{3,2,1,0:T(8,128)(2,1)S(1)} %own.1), channel_id=1, replica_groups=mesh['rep'=16,'gx'=4,'gy'=8] {'rep'}, dimensions={0} | all-to-all | bytes 1048576 | tf_op jit(solution)/shard_map/all_to_all | solution.py:368
  40.6 0.0 copy-done.2
  40.6 0.6 pick.1
  41.2 0.0 copy-done
  41.2 37.1 %all-gather.2 = f16[48,4,32,128]{3,2,1,0:T(8,128)(2,1)S(1)} all-gather(f16[3,4,32,128]{3,2,1,0:T(8,128)(2,1)S(1)} %convert_element_type.6), channel_id=2, replica_groups=mesh['rep'=16,'gx'=4,'gy'=8] {'rep'}, dimensions={0}, use_global_device_ids=true | all-gather | bytes 1671168 | tf_op jit(solution)/shard_map/all_gather | solution.py:377
  78.3 0.3 convert_element_type.7.lev_ref
  78.7 0.0 copy-start.1
  78.8 12.2 %collective-permute-start.1 = (bf16[18,32,128]{2,1,0:T(8,128)(2,1)S(1)}, bf16[18,32,128]{2,1,0:T(8,128)(2,1)S(1)}, u32[]{:S(2)}, u32[]{:S(2)}) collective-permute-start(bf16[18,32,128]{2,1,0:T(8,128)(2,1)S(1)} %get-tuple-element.26), channel_id=1, source_target_pairs={{8,0},{16,8},{24,16},{9,1},{17,9},{25,17},{10,2},{18,10},{26,18},{... | collective-permute-start | bytes 442376 | tf_op jit(solution)/shard_map/ppermute | solution.py:347
  91.1 3.0 %collective-permute-start = (bf16[18,32,128]{2,1,0:T(8,128)(2,1)S(1)}, bf16[18,32,128]{2,1,0:T(8,128)(2,1)S(1)}, u32[]{:S(2)}, u32[]{:S(2)}) collective-permute-start(bf16[18,32,128]{2,1,0:T(8,128)(2,1)S(1)} %get-tuple-element.27), channel_id=1, source_target_pairs={{0,8},{8,16},{16,24},{1,9},{9,17},{17,25},{2,10},{10,18},{18,26},{... | collective-permute-start | bytes 442376 | tf_op jit(solution)/shard_map/ppermute | solution.py:346
  94.1 0.9 collective-permute-done.1.down_ref
  95.0 1.2 collective-permute-done.up_ref
  96.2 0.3 pack.1
  96.5 0.7 collective-permute-start.2
  97.2 7.1 %collective-permute-start.3 = (bf16[608,128]{1,0:T(8,128)(2,1)S(1)}, bf16[608,128]{1,0:T(8,128)(2,1)S(1)}, u32[]{:S(2)}, u32[]{:S(2)}) collective-permute-start(bf16[608,128]{1,0:T(8,128)(2,1)S(1)} %get-tuple-element.20), channel_id=1, source_target_pairs={{0,1},{1,0},{2,3},{3,2},{4,5},{5,4},{6,7},{7,6},{8,9},{9,8},{10,11... | collective-permute-start | bytes 466952 | tf_op jit(solution)/shard_map/ppermute | solution.py:52
  104.3 0.0 copy-done.1
  104.3 7.3 %inner.1 = (f32[3,1024,128]{2,1,0:T(8,128)}, f32[1024,128]{1,0:T(8,128)S(1)}, f32[2,3,6,38,128]{4,3,2,1,0:T(8,128)S(1)}, f32[2,3,4,6,38,128]{5,4,3,2,1,0:T(8,128)S(1)}, f32[2,3,256,128]{3,2,1,0:T(8,128)S(1)}) custom-call(f32[3]{0:T(128)S(1)} %copy-done.1, bf16[3,32,32,128]{3,2,1,0:T(8,128)(2,1)S(1)} %copy-done, ...), custom_call_target="tpu_custom_call" | custom-call | tf_op jit(solution)/shard_map/inner/pallas_call | solution.py:415
  111.6 0.0 collective-permute-done.2.odd_ref
  111.7 0.0 collective-permute-done.3.even_ref
  111.7 2.7 %edge.1 = (f32[2,3,256,128]{3,2,1,0:T(8,128)S(1)}, f32[3,32,32,128]{3,2,1,0:T(8,128)}, f32[1024,128]{1,0:T(8,128)S(1)}) custom-call(f32[3]{0:T(128)S(1)} %copy-done.1, f32[2,3,6,38,128]{4,3,2,1,0:T(8,128)S(1)} %get-tuple-element.17.edge_state, ...), custom_call_target="tpu_custom_call", output_to_operand_aliasing={{0}: (5, {}), {1}: (6, {}), {2}: (7, {})} | custom-call | tf_op jit(solution)/shard_map/edge/pallas_call | solution.py:434
  114.4 32.8 %all_to_all.11 = f32[16,2,32,128]{3,2,1,0:T(8,128)S(1)} all-to-all(f32[16,2,32,128]{3,2,1,0:T(8,128)S(1)} %bitcast.77), channel_id=1, replica_groups=mesh['rep'=16,'gx'=4,'gy'=8] {'rep'}, dimensions={0} | all-to-all | bytes 1048576 | tf_op jit(solution)/shard_map/all_to_all | solution.py:452
  147.2 0.6 reduce_sum.9
  (12 shorter events, 0.1 us)
Async XLA Ops:
  0.6 40.0 %copy-start.2 = (s32[3]{0:T(128)S(1)}, s32[3]{0:T(128)}, u32[]{:S(2)}) copy-start(s32[3]{0:T(128)} %levels_ref) | copy-start | bytes 40
  0.6 40.6 %copy-start = (bf16[3,32,32,128]{3,2,1,0:T(8,128)(2,1)S(1)}, bf16[3,32,32,128]{3,2,1,0:T(8,128)(2,1)}, u32[]{:S(2)}) copy-start(bf16[3,32,32,128]{3,2,1,0:T(8,128)(2,1)} %f_ref.1) | copy-start | bytes 2359300
  78.7 25.6 %copy-start.1 = (f32[3]{0:T(128)S(1)}, f32[3]{0:T(128)}, u32[]{:S(2)}) copy-start(f32[3]{0:T(128)} %coef_ref.3) | copy-start | bytes 40
  78.8 16.2 %collective-permute-start.1 = (bf16[18,32,128]{2,1,0:T(8,128)(2,1)S(1)}, bf16[18,32,128]{2,1,0:T(8,128)(2,1)S(1)}, u32[]{:S(2)}, u32[]{:S(2)}) collective-permute-start(bf16[18,32,128]{2,1,0:T(8,128)(2,1)S(1)} %get-tuple-element.26), channel_id=1, source_target_pairs={{8,0},{16,8},{24,16},{9,1},{17,9},{25,17},{10,2},{18,10},{26,18},{... | collective-permute-start | bytes 442376 | tf_op jit(solution)/shard_map/ppermute | solution.py:347
  91.1 5.1 %collective-permute-start = (bf16[18,32,128]{2,1,0:T(8,128)(2,1)S(1)}, bf16[18,32,128]{2,1,0:T(8,128)(2,1)S(1)}, u32[]{:S(2)}, u32[]{:S(2)}) collective-permute-start(bf16[18,32,128]{2,1,0:T(8,128)(2,1)S(1)} %get-tuple-element.27), channel_id=1, source_target_pairs={{0,8},{8,16},{16,24},{1,9},{9,17},{17,25},{2,10},{10,18},{18,26},{... | collective-permute-start | bytes 442376 | tf_op jit(solution)/shard_map/ppermute | solution.py:346
  96.5 15.2 %collective-permute-start.2 = (bf16[608,128]{1,0:T(8,128)(2,1)S(1)}, bf16[608,128]{1,0:T(8,128)(2,1)S(1)}, u32[]{:S(2)}, u32[]{:S(2)}) collective-permute-start(bf16[608,128]{1,0:T(8,128)(2,1)S(1)} %get-tuple-element.19), channel_id=1, source_target_pairs={{1,2},{2,1},{3,4},{4,3},{5,6},{6,5},{9,10},{10,9},{11,12},{12,11},... | collective-permute-start | bytes 466952 | tf_op jit(solution)/shard_map/ppermute | solution.py:52
  97.2 14.5 %collective-permute-start.3 = (bf16[608,128]{1,0:T(8,128)(2,1)S(1)}, bf16[608,128]{1,0:T(8,128)(2,1)S(1)}, u32[]{:S(2)}, u32[]{:S(2)}) collective-permute-start(bf16[608,128]{1,0:T(8,128)(2,1)S(1)} %get-tuple-element.20), channel_id=1, source_target_pairs={{0,1},{1,0},{2,3},{3,2},{4,5},{5,4},{6,7},{7,6},{8,9},{9,8},{10,11... | collective-permute-start | bytes 466952 | tf_op jit(solution)/shard_map/ppermute | solution.py:52

commit v6 on v5

--- a/solution.py
+++ b/solution.py
@@ -258,7 +258,7 @@
 
 def edge_kernel(
     reps, rows, cols,
-    coef_ref, edge_state, edge_terms, odd_ref, even_ref, tiles_in, adj_in, sum_in,
+    coef_ref, edge_state, edge_terms, even_ref, odd_ref, tiles_in, adj_in, sum_in,
     tiles, adj_hbm, sum_ref,
     got, halo_state, halo_terms, state, spare, sems,
 ):
@@ -447,7 +447,7 @@
         input_output_aliases={5: 0, 6: 1, 7: 2},
         compiler_params=pltpu.CompilerParams(vmem_limit_bytes=12 * 2**20),
         name="edge",
-    )(coefficients, edge_state, edge_terms, odd, even, tiles, adjoints, weighted)
+    )(coefficients, edge_state, edge_terms, even, odd, tiles, adjoints, weighted)
 
     parts = lax.all_to_all(weighted.reshape(groups, own, cols, lanes), "rep", 0, 0, tiled=True)
     return jnp.sum(parts, axis=0), adjoints

time: 148 us -> 147 us (level)
  the two profiles are of different devices: /device:TPU:1 before, /device:TPU:13 now
where the time goes in v6:
time: 147 us
  blocking collectives  108 us (73%)
  starting transfers between devices  22.8 us (16%)
  Pallas kernels  12.2 us (8%)
  waiting for transfers between devices  2.08 us (1%)
    all_to_all x1, blocking collectives, local(): slices = lax.all_to_all(mine, 'rep', 0, 0, tiled=True)  37.7 us
    all_gather x1, blocking collectives, local(): lev = lax.all_gather(picked.astype(jnp.float16), 'rep', axis=0, tiled=False)  37.1 us
    all_to_all x1, blocking collectives, local(): lax.all_to_all(weighted.reshape(groups, own, cols, lanes), 'rep', 0, 0, t...  32.8 us
    ppermute x1, starting transfers between devices, shift(): return lax.ppermute(x, axis, [(i + 1, i) for i in range(n - 1)])  12.2 us
    ppermute x2, starting transfers between devices, swaps(): lax.ppermute(x, axis, [p for i in range(first, ends, 2) for p in ((i, i +...  7.8 us
    pallas_call x1, Pallas kernels, local(): pl.pallas_call(functools.partial(inner_kernel, reps, rows, cols), out_sha...  7.32 us
  transfers between devices with their start and end apart: 4, of which 2 were waited for; matrix products, arithmetic and copies ran while one was open for 0% of the time, Pallas kernels for 5%

profile of v6, /device:TPU:13, one launch (start us, length us, event | category | flops | bytes accessed | tf_op | source)
XLA Modules:
  0.0 146.7 jit_solution(8004566794145517637)
XLA Ops:
  0.6 0.0 copy-start.2
  0.6 0.0 copy-start
  0.7 1.4 own.1
  2.1 37.7 %all_to_all.10.slices_ref = bf16[16,4,32,128]{3,2,1,0:T(8,128)(2,1)S(1)} all-to-all(bf16[16,4,32,128]{3,2,1,0:T(8,128)(2,1)S(1)} %own.1), channel_id=1, replica_groups=mesh['rep'=16,'gx'=4,'gy'=8] {'rep'}, dimensions={0} | all-to-all | bytes 1048576 | tf_op jit(solution)/shard_map/all_to_all | solution.py:368
  39.8 0.0 copy-done.2
  39.8 0.6 pick.1
  40.4 0.0 copy-done
  40.4 37.1 %all-gather.2 = f16[48,4,32,128]{3,2,1,0:T(8,128)(2,1)S(1)} all-gather(f16[3,4,32,128]{3,2,1,0:T(8,128)(2,1)S(1)} %convert_element_type.6), channel_id=2, replica_groups=mesh['rep'=16,'gx'=4,'gy'=8] {'rep'}, dimensions={0}, use_global_device_ids=true | all-gather | bytes 1671168 | tf_op jit(solution)/shard_map/all_gather | solution.py:377
  77.5 0.3 convert_element_type.7.lev_ref
  77.9 0.0 copy-start.1
  78.0 12.2 %collective-permute-start.1 = (bf16[18,32,128]{2,1,0:T(8,128)(2,1)S(1)}, bf16[18,32,128]{2,1,0:T(8,128)(2,1)S(1)}, u32[]{:S(2)}, u32[]{:S(2)}) collective-permute-start(bf16[18,32,128]{2,1,0:T(8,128)(2,1)S(1)} %get-tuple-element.26), channel_id=1, source_target_pairs={{8,0},{16,8},{24,16},{9,1},{17,9},{25,17},{10,2},{18,10},{26,18},{... | collective-permute-start | bytes 442376 | tf_op jit(solution)/shard_map/ppermute | solution.py:347
  90.3 2.7 %collective-permute-start = (bf16[18,32,128]{2,1,0:T(8,128)(2,1)S(1)}, bf16[18,32,128]{2,1,0:T(8,128)(2,1)S(1)}, u32[]{:S(2)}, u32[]{:S(2)}) collective-permute-start(bf16[18,32,128]{2,1,0:T(8,128)(2,1)S(1)} %get-tuple-element.27), channel_id=1, source_target_pairs={{0,8},{8,16},{16,24},{1,9},{9,17},{17,25},{2,10},{10,18},{18,26},{... | collective-permute-start | bytes 442376 | tf_op jit(solution)/shard_map/ppermute | solution.py:346
  93.0 0.9 collective-permute-done.1.down_ref
  93.9 1.2 collective-permute-done.up_ref
  95.1 0.3 pack.1
  95.4 2.4 %collective-permute-start.2 = (bf16[608,128]{1,0:T(8,128)(2,1)S(1)}, bf16[608,128]{1,0:T(8,128)(2,1)S(1)}, u32[]{:S(2)}, u32[]{:S(2)}) collective-permute-start(bf16[608,128]{1,0:T(8,128)(2,1)S(1)} %get-tuple-element.19), channel_id=1, source_target_pairs={{0,1},{1,0},{2,3},{3,2},{4,5},{5,4},{6,7},{7,6},{8,9},{9,8},{10,11... | collective-permute-start | bytes 466952 | tf_op jit(solution)/shard_map/ppermute | solution.py:52
  97.8 5.4 %collective-permute-start.3 = (bf16[608,128]{1,0:T(8,128)(2,1)S(1)}, bf16[608,128]{1,0:T(8,128)(2,1)S(1)}, u32[]{:S(2)}, u32[]{:S(2)}) collective-permute-start(bf16[608,128]{1,0:T(8,128)(2,1)S(1)} %get-tuple-element.20), channel_id=1, source_target_pairs={{1,2},{2,1},{3,4},{4,3},{5,6},{6,5},{9,10},{10,9},{11,12},{12,11},... | collective-permute-start | bytes 466952 | tf_op jit(solution)/shard_map/ppermute | solution.py:52
  103.2 0.0 copy-done.1
  103.2 7.3 %inner.1 = (f32[3,1024,128]{2,1,0:T(8,128)}, f32[1024,128]{1,0:T(8,128)S(1)}, f32[2,3,6,38,128]{4,3,2,1,0:T(8,128)S(1)}, f32[2,3,4,6,38,128]{5,4,3,2,1,0:T(8,128)S(1)}, f32[2,3,256,128]{3,2,1,0:T(8,128)S(1)}) custom-call(f32[3]{0:T(128)S(1)} %copy-done.1, bf16[3,32,32,128]{3,2,1,0:T(8,128)(2,1)S(1)} %copy-done, ...), custom_call_target="tpu_custom_call" | custom-call | tf_op jit(solution)/shard_map/inner/pallas_call | solution.py:415
  110.5 0.0 collective-permute-done.2.even_ref
  110.5 0.0 collective-permute-done.3.odd_ref
  110.6 2.7 %edge.1 = (f32[2,3,256,128]{3,2,1,0:T(8,128)S(1)}, f32[3,32,32,128]{3,2,1,0:T(8,128)}, f32[1024,128]{1,0:T(8,128)S(1)}) custom-call(f32[3]{0:T(128)S(1)} %copy-done.1, f32[2,3,6,38,128]{4,3,2,1,0:T(8,128)S(1)} %get-tuple-element.17.edge_state, ...), custom_call_target="tpu_custom_call", output_to_operand_aliasing={{0}: (5, {}), {1}: (6, {}), {2}: (7, {})} | custom-call | tf_op jit(solution)/shard_map/edge/pallas_call | solution.py:434
  113.2 32.8 %all_to_all.11 = f32[16,2,32,128]{3,2,1,0:T(8,128)S(1)} all-to-all(f32[16,2,32,128]{3,2,1,0:T(8,128)S(1)} %bitcast.77), channel_id=1, replica_groups=mesh['rep'=16,'gx'=4,'gy'=8] {'rep'}, dimensions={0} | all-to-all | bytes 1048576 | tf_op jit(solution)/shard_map/all_to_all | solution.py:452
  146.0 0.6 reduce_sum.9
  (12 shorter events, 0.1 us)
Async XLA Ops:
  0.6 39.1 %copy-start.2 = (s32[3]{0:T(128)S(1)}, s32[3]{0:T(128)}, u32[]{:S(2)}) copy-start(s32[3]{0:T(128)} %levels_ref) | copy-start | bytes 40
  0.6 39.7 %copy-start = (bf16[3,32,32,128]{3,2,1,0:T(8,128)(2,1)S(1)}, bf16[3,32,32,128]{3,2,1,0:T(8,128)(2,1)}, u32[]{:S(2)}) copy-start(bf16[3,32,32,128]{3,2,1,0:T(8,128)(2,1)} %f_ref.1) | copy-start | bytes 2359300
  77.9 25.3 %copy-start.1 = (f32[3]{0:T(128)S(1)}, f32[3]{0:T(128)}, u32[]{:S(2)}) copy-start(f32[3]{0:T(128)} %coef_ref.3) | copy-start | bytes 40
  78.0 15.9 %collective-permute-start.1 = (bf16[18,32,128]{2,1,0:T(8,128)(2,1)S(1)}, bf16[18,32,128]{2,1,0:T(8,128)(2,1)S(1)}, u32[]{:S(2)}, u32[]{:S(2)}) collective-permute-start(bf16[18,32,128]{2,1,0:T(8,128)(2,1)S(1)} %get-tuple-element.26), channel_id=1, source_target_pairs={{8,0},{16,8},{24,16},{9,1},{17,9},{25,17},{10,2},{18,10},{26,18},{... | collective-permute-start | bytes 442376 | tf_op jit(solution)/shard_map/ppermute | solution.py:347
  90.3 4.8 %collective-permute-start = (bf16[18,32,128]{2,1,0:T(8,128)(2,1)S(1)}, bf16[18,32,128]{2,1,0:T(8,128)(2,1)S(1)}, u32[]{:S(2)}, u32[]{:S(2)}) collective-permute-start(bf16[18,32,128]{2,1,0:T(8,128)(2,1)S(1)} %get-tuple-element.27), channel_id=1, source_target_pairs={{0,8},{8,16},{16,24},{1,9},{9,17},{17,25},{2,10},{10,18},{18,26},{... | collective-permute-start | bytes 442376 | tf_op jit(solution)/shard_map/ppermute | solution.py:346
  95.4 15.2 %collective-permute-start.2 = (bf16[608,128]{1,0:T(8,128)(2,1)S(1)}, bf16[608,128]{1,0:T(8,128)(2,1)S(1)}, u32[]{:S(2)}, u32[]{:S(2)}) collective-permute-start(bf16[608,128]{1,0:T(8,128)(2,1)S(1)} %get-tuple-element.19), channel_id=1, source_target_pairs={{0,1},{1,0},{2,3},{3,2},{4,5},{5,4},{6,7},{7,6},{8,9},{9,8},{10,11... | collective-permute-start | bytes 466952 | tf_op jit(solution)/shard_map/ppermute | solution.py:52
  97.8 12.7 %collective-permute-start.3 = (bf16[608,128]{1,0:T(8,128)(2,1)S(1)}, bf16[608,128]{1,0:T(8,128)(2,1)S(1)}, u32[]{:S(2)}, u32[]{:S(2)}) collective-permute-start(bf16[608,128]{1,0:T(8,128)(2,1)S(1)} %get-tuple-element.20), channel_id=1, source_target_pairs={{1,2},{2,1},{3,4},{4,3},{5,6},{6,5},{9,10},{10,9},{11,12},{12,11},... | collective-permute-start | bytes 466952 | tf_op jit(solution)/shard_map/ppermute | solution.py:52
